TPU v7x, 32 devices: a whole 2x2x4 slice. The times are simulated.
32 devices in a mesh: row: 8 (over y, x, core), col: 4 (over z).
Axes of the slice: x: 2, y: 2, z: 4, core: 2. Of those that a mesh axis runs over, the one named last changes fastest.
Arguments:
- resident_inverse: bfloat16 [24576, 24576], P('row', 'col')
- factor: bfloat16 [3, 24576, 512], P(None, 'row', 'col'), may hold values from -0.15625 to 0.15625
- diag_inverse: float32 [3, 512, 512], P(None, None, 'col'), may hold values from -4 to 4
- anc_tiles: int32 [3, 64], replicated, may hold values from -1 to 95, as said below
- slot_tile: int32 [96], replicated, may hold values from 0 to 95, as said below
Outputs:
- new_cols: bfloat16 [3, 24576, 512], P(None, 'row', 'col')
- diag_blocks: float32 [3, 512, 512], P(None, None, 'col')
Inputs may be any that keep to these rules, and one draw needn't show every extreme that they name: `anc_tiles`: row j lists the ancestor tiles of supernode j in ascending order, each at most once, followed by -1 in unused entries; every list holds tile 96 - 1; list 0 is full and list 2 has fewer than 32 tiles. A permutation of the tiles; slot s holds tile slot_tile[s], and each tile is stored within the same block of 24 consecutive slots as its own index. `resident_inverse` is symmetric. `resident_inverse` is symmetric.
All inputs are finite; a program needn't handle non-finite values.
Results may differ from a plain program's by a relative error of at most 0.017.
Values may be sent and summed in bfloat16 or wider, within the bound.
A program may use at most 128 MiB of HBM per device.

v0:
```python
import jax
import jax.numpy as jnp
from jax import lax
from jax.sharding import PartitionSpec as P


def slot_rows(anc_tiles, slot_tile, tile_rows):
    listed = (anc_tiles[:, :, None] == slot_tile[None, None, :]).any(axis=1)
    return jnp.repeat(listed.astype(jnp.float32), tile_rows, axis=1)


def on_device(resident_inverse, factor, diag_inverse, anc_tiles, slot_tile):
    own_rows = resident_inverse.shape[0]
    supers, _, part_width = factor.shape
    row_index = lax.axis_index("row")
    col_count = lax.axis_size("col")
    row_count = lax.axis_size("row")
    ratio = row_count // col_count
    total_rows = own_rows * row_count
    row_mask = slot_rows(anc_tiles, slot_tile, total_rows // slot_tile.shape[0])
    own_mask = lax.dynamic_slice_in_dim(row_mask, row_index * own_rows, own_rows, 1)
    mine = factor * own_mask.astype(jnp.bfloat16)[:, :, None]
    chunk = own_rows // row_count
    spread = mine.reshape(supers, row_count, chunk, part_width).transpose(1, 0, 2, 3)
    spread = lax.all_to_all(spread, "row", 0, 0, tiled=True)
    spread = spread.reshape(col_count, ratio * supers * chunk, part_width)
    spread = lax.all_to_all(spread, "col", 0, 0, tiled=True)
    spread = spread.reshape(col_count, ratio, supers, chunk, part_width)
    spread = spread.transpose(2, 1, 3, 0, 4).reshape(supers, ratio, chunk, col_count * part_width)
    spread, later = lax.optimization_barrier((spread, mine))
    col_index = lax.axis_index("col")

    last = col_count - 1
    up_moves = [(i, i + 1) for i in range(last)]
    down_moves = [(i + 1, i) for i in range(last)]

    def up(value):
        return lax.ppermute(value, "col", up_moves)

    def down(value):
        return lax.ppermute(value, "col", down_moves)

    gathered = [lax.all_gather(spread[s], "row", axis=1, tiled=True) for s in range(supers)]
    ups, downs = [later], [later]
    for by in range(last):
        low, high = ups[-1], downs[-1]
        if 0 < by <= supers:
            gathered[by - 1], low, high = lax.optimization_barrier((gathered[by - 1], low, high))
        ups.append(up(low))
        downs.append(down(high))
    partials = []
    for s in range(supers):
        blocks = gathered[s].reshape(ratio * own_rows, col_count * part_width)
        partials.append(
            jnp.dot(resident_inverse, blocks, preferred_element_type=jnp.float32).astype(jnp.bfloat16)
        )

    def piece(s, to):
        to = jnp.clip(to, 0, last) * part_width
        return lax.dynamic_slice_in_dim(partials[s], to, part_width, 1)

    kept = [piece(s, col_index) for s in range(supers)]
    kept[-1], ups, downs = lax.optimization_barrier((kept[-1], ups, downs))
    others = [later] + [ups[by] + downs[col_count - by] for by in range(1, col_count)]
    news, contribs = [], []
    for s in range(supers):
        from_below = piece(s, col_index + last)
        from_above = piece(s, col_index - last)
        for by in range(last, 0, -1):
            from_below, from_above = up(from_below), down(from_above)
            if by > 1:
                from_below = from_below + piece(s, col_index + by - 1)
                from_above = from_above + piece(s, col_index - by + 1)
        summed = (
            kept[s].astype(jnp.float32)
            + from_below.astype(jnp.float32)
            + from_above.astype(jnp.float32)
        )
        news.append((-(summed * own_mask[s][:, None])).astype(jnp.bfloat16))
        summed = summed.astype(jnp.bfloat16)
        contribs.append(jnp.stack([
            jnp.einsum("rw,rv->wv", other[s], summed, preferred_element_type=jnp.float32)
            for other in others
        ]))
    stacked = jnp.stack(contribs, axis=1)
    ordered = jnp.stack([
        lax.dynamic_index_in_dim(stacked, (col_index - q) % col_count, 0, keepdims=False)
        for q in range(col_count)
    ], axis=1)
    totals = ordered.reshape(supers, col_count * part_width, part_width)
    step = 1
    while step < row_count:
        sent = totals.astype(jnp.bfloat16)
        got = lax.ppermute(sent, "row", [(i, i ^ step) for i in range(row_count)])
        totals = sent.astype(jnp.float32) + got.astype(jnp.float32)
        step *= 2
    return (jnp.stack(news), diag_inverse + totals)


def solution(mesh):
    placed = (P("row", "col"), P(None, "row", "col"), P(None, None, "col"), P(), P())
    return jax.shard_map(
        on_device,
        mesh=mesh,
        in_specs=placed,
        out_specs=(P(None, "row", "col"), P(None, None, "col")),
        check_vma=False,
    )
```

profile of v0, /device:TPU:0, one launch (start us, length us, event | category | flops | bytes accessed | tf_op | source)
XLA Modules:
  0.0 506.3 jit_solution(2496138775720817492)
XLA Ops:
  7.2 0.8 compare_reduce_fusion
  8.4 3.3 broadcast_multiply_fusion
  11.9 34.4 %all_to_all.10 = bf16[8,3,384,128]{3,2,1,0:T(8,128)(2,1)S(1)} all-to-all(bf16[8,3,384,128]{3,2,1,0:T(8,128)(2,1)S(1)} %copy.37), channel_id=1, replica_groups=mesh['row'=8,'col'=4] {'row'}, dimensions={0} | all-to-all | bytes 4718592 | tf_op jit(solution)/shard_map/all_to_all | solution.py:25
  46.2 58.0 %all_to_all.11 = bf16[4,2304,128]{2,1,0:T(8,128)(2,1)} all-to-all(bf16[4,2304,128]{2,1,0:T(8,128)(2,1)S(1)} %bitcast.191), channel_id=1, replica_groups=mesh['row'=8,'col'=4] {'col'}, dimensions={0} | all-to-all | bytes 4718592 | tf_op jit(solution)/shard_map/all_to_all | solution.py:27
  104.3 4.3 copy.38
  108.6 3.1 fusion.18
  112.5 1.3 collective-permute-start.1
  113.8 6.0 %collective-permute-start = (bf16[3,3072,128]{2,1,0:T(8,128)(2,1)S(1)}, bf16[3,3072,128]{2,1,0:T(8,128)(2,1)}, u32[]{:S(2)}, u32[]{:S(2)}) collective-permute-start(bf16[3,3072,128]{2,1,0:T(8,128)(2,1)S(1)} %broadcast_multiply_fusion), channel_id=1, source_target_pairs={{0,1},{1,2},{2,3},{4,5},{5,6},{6,7},{8,9},{9,10},{10,11},{12,13},{... | collective-permute-start | bytes 7077896 | tf_op jit(solution)/shard_map/ppermute | solution.py:38
  119.9 0.7 constant_dynamic-slice_fusion
  120.6 45.6 %collective-permute-done.1 = bf16[3,3072,128]{2,1,0:T(8,128)(2,1)} collective-permute-done((bf16[3,3072,128]{2,1,0:T(8,128)(2,1)S(1)}, bf16[3,3072,128]{2,1,0:T(8,128)(2,1)}, u32[]{:S(2)}, u32[]{:S(2)}) %collective-permute-start.1) | collective-permute-done | bytes 2359328 | tf_op jit(solution)/shard_map/ppermute | solution.py:41
  166.2 1.1 collective-permute-done
  167.3 8.8 %copy.39 = bf16[2,3072,512]{2,1,0:T(8,128)(2,1)} copy(bf16[2,3072,512]{1,2,0:T(8,128)(2,1)} %bitcast.194) | data formatting | bytes 12582912 | tf_op jit(solution)/shard_map/optimization_barrier | solution.py:48
  176.0 25.9 %convolution_convert_fusion.2 = bf16[512,3072]{1,0:T(8,128)(2,1)S(1)} fusion(bf16[6144,512]{1,0:T(8,128)(2,1)} %bitcast.195, bf16[3072,6144]{1,0:T(8,128)(2,1)} %param.5), kind=kOutput, calls=%fused_computation.2 | convolution fusion | flops 19328925696 | bytes 47185920 | tf_op jit(solution)/shard_map/dot_general | solution.py:55
  201.9 1.4 dynamic-slice_bitcast_fusion.6
  203.3 5.4 %collective-permute-start.2 = (bf16[3072,128]{0,1:T(8,128)(2,1)}, bf16[3072,128]{0,1:T(8,128)(2,1)}, u32[]{:S(2)}, u32[]{:S(2)}) collective-permute-start(bf16[3072,128]{0,1:T(8,128)(2,1)} %get-tuple-element.50), channel_id=1, source_target_pairs={{0,1},{1,2},{2,3},{4,5},{5,6},{6,7},{8,9},{9,10},{10,11},{12,13},{... | collective-permute-start | bytes 2359304 | tf_op jit(solution)/shard_map/ppermute | solution.py:38
  208.7 1.3 collective-permute-start.5
  209.9 6.0 %collective-permute-start.8 = (bf16[3,3072,128]{2,1,0:T(8,128)(2,1)}, bf16[3,3072,128]{2,1,0:T(8,128)(2,1)}, u32[]{:S(2)}, u32[]{:S(2)}) collective-permute-start(bf16[3,3072,128]{2,1,0:T(8,128)(2,1)} %collective-permute-done), channel_id=1, source_target_pairs={{0,1},{1,2},{2,3},{4,5},{5,6},{6,7},{8,9},{9,10},{10,11},{12,13},{... | collective-permute-start | bytes 7077896 | tf_op jit(solution)/shard_map/ppermute | solution.py:38
  216.0 1.7 collective-permute-start.9
  217.8 8.7 %copy.41 = bf16[1,2,3072,512]{3,2,1,0:T(8,128)(2,1)} copy(bf16[1,2,3072,512]{2,3,1,0:T(8,128)(2,1)} %all-gather.11.cloned.1.call-done) | data formatting | bytes 12582912 | tf_op jit(solution)/shard_map/all_gather | solution.py:43
  226.4 28.4 %convolution_convert_fusion = bf16[512,3072]{1,0:T(8,128)(2,1)} fusion(bf16[6144,512]{1,0:T(8,128)(2,1)} %bitcast.196, bf16[3072,6144]{1,0:T(8,128)(2,1)} %param.5), kind=kOutput, calls=%fused_computation | convolution fusion | flops 19328925696 | bytes 47185920 | tf_op jit(solution)/shard_map/dot_general | solution.py:55
  254.8 3.1 dynamic-slice_bitcast_fusion.2
  257.9 1.3 collective-permute-start.21
  259.2 6.2 %collective-permute-start.18 = (bf16[3072,128]{0,1:T(8,128)(2,1)}, bf16[3072,128]{0,1:T(8,128)(2,1)}, u32[]{:S(2)}, u32[]{:S(2)}) collective-permute-start(bf16[3072,128]{0,1:T(8,128)(2,1)} %get-tuple-element.60), channel_id=1, source_target_pairs={{0,1},{1,2},{2,3},{4,5},{5,6},{6,7},{8,9},{9,10},{10,11},{12,13},{... | collective-permute-start | bytes 2359304 | tf_op jit(solution)/shard_map/ppermute | solution.py:38
  265.4 3.1 bitcast_add_fusion.13
  268.4 4.0 collective-permute-start.3
  272.4 4.1 collective-permute-done.8
  276.5 1.5 collective-permute-start.6
  278.0 3.8 collective-permute-done.9
  281.8 8.7 %copy.40 = bf16[2,3072,512]{2,1,0:T(8,128)(2,1)} copy(bf16[2,3072,512]{1,2,0:T(8,128)(2,1)} %bitcast.193) | data formatting | bytes 12582912 | tf_op jit(solution)/shard_map/optimization_barrier | solution.py:48
  290.6 25.9 %convolution_convert_fusion.1 = bf16[512,3072]{1,0:T(8,128)(2,1)S(1)} fusion(bf16[6144,512]{1,0:T(8,128)(2,1)} %bitcast.197, bf16[3072,6144]{1,0:T(8,128)(2,1)} %param.5), kind=kOutput, calls=%fused_computation.1 | convolution fusion | flops 19328925696 | bytes 47185920 | tf_op jit(solution)/shard_map/dot_general | solution.py:55
  316.6 2.0 collective-permute-start.10
  318.6 1.6 collective-permute-start.13
  320.2 1.9 bitcast_add_fusion.5
  322.1 4.6 collective-permute-start.19
  326.7 1.3 collective-permute-start.22
  328.0 2.0 bitcast_add_fusion.12
  330.0 4.6 collective-permute-start.4
  334.6 1.9 collective-permute-done.10
  336.5 1.3 collective-permute-start.7
  337.8 3.4 collective-permute-done.13
  341.2 4.0 collective-permute-start.16
  345.8 7.5 %collective-permute-done.19 = bf16[3072,128]{0,1:T(8,128)(2,1)S(1)} collective-permute-done((bf16[3072,128]{0,1:T(8,128)(2,1)S(1)}, bf16[3072,128]{0,1:T(8,128)(2,1)S(1)}, u32[]{:S(2)}, u32[]{:S(2)}) %collective-permute-start.19) | collective-permute-done | bytes 786464 | tf_op jit(solution)/shard_map/ppermute | solution.py:38
  353.3 1.3 collective-permute-start.17
  354.6 3.4 collective-permute-done.22
  358.1 3.9 collective-permute-start.11
  362.5 7.7 %collective-permute-done.4 = bf16[3072,128]{0,1:T(8,128)(2,1)S(1)} collective-permute-done((bf16[3072,128]{0,1:T(8,128)(2,1)S(1)}, bf16[3072,128]{0,1:T(8,128)(2,1)S(1)}, u32[]{:S(2)}, u32[]{:S(2)}) %collective-permute-start.4) | collective-permute-done | bytes 786464 | tf_op jit(solution)/shard_map/ppermute | solution.py:38
  370.2 4.4 collective-permute-start.20
  374.9 1.3 collective-permute-start.14
  376.7 60.9 %collective-permute-done.11 = bf16[3072,128]{0,1:T(8,128)(2,1)S(1)} collective-permute-done((bf16[3072,128]{0,1:T(8,128)(2,1)S(1)}, bf16[3072,128]{0,1:T(8,128)(2,1)S(1)}, u32[]{:S(2)}, u32[]{:S(2)}) %collective-permute-start.11) | collective-permute-done | bytes 786464 | tf_op jit(solution)/shard_map/ppermute | solution.py:38
  437.6 1.3 collective-permute-start.23
  439.3 1.8 collective-permute-done.14
  441.7 3.3 collective-permute-start.12
  445.0 1.5 collective-permute-start.15
  446.5 7.9 %collective-permute-done.20 = bf16[3072,128]{0,1:T(8,128)(2,1)S(1)} collective-permute-done((bf16[3072,128]{0,1:T(8,128)(2,1)S(1)}, bf16[3072,128]{0,1:T(8,128)(2,1)S(1)}, u32[]{:S(2)}, u32[]{:S(2)}) %collective-permute-start.20) | collective-permute-done | bytes 786464 | tf_op jit(solution)/shard_map/ppermute | solution.py:38
  454.4 5.9 %collective-permute-done.23 = bf16[3072,128]{0,1:T(8,128)(2,1)S(1)} collective-permute-done((bf16[3072,128]{0,1:T(8,128)(2,1)S(1)}, bf16[3072,128]{0,1:T(8,128)(2,1)S(1)}, u32[]{:S(2)}, u32[]{:S(2)}) %collective-permute-start.23) | collective-permute-done | bytes 786464 | tf_op jit(solution)/shard_map/ppermute | solution.py:41
  461.3 2.3 add.202
  464.0 3.0 add.203
  467.4 2.3 add.204
  473.9 1.7 collective-permute-done.24
  475.7 1.4 collective-permute-start.25
  477.2 9.8 %collective-permute-done.25 = bf16[3,512,128]{2,1,0:T(8,128)(2,1)S(1)} collective-permute-done((bf16[3,512,128]{2,1,0:T(8,128)(2,1)S(1)}, bf16[3,512,128]{2,1,0:T(8,128)(2,1)S(1)}, u32[]{:S(2)}, u32[]{:S(2)}) %collective-permute-start.25) | collective-permute-done | bytes 393248 | tf_op jit(solution)/shard_map/ppermute | solution.py:94
  488.0 2.4 copy.46
  490.4 7.1 %collective-permute-done.26 = bf16[3,512,128]{2,1,0:T(8,128)(2,1)} collective-permute-done((bf16[3,512,128]{2,1,0:T(8,128)(2,1)S(1)}, bf16[3,512,128]{2,1,0:T(8,128)(2,1)}, u32[]{:S(2)}, u32[]{:S(2)}) %collective-permute-start.26) | collective-permute-done | bytes 393248 | tf_op jit(solution)/shard_map/ppermute | solution.py:94
  497.5 2.0 add_add_fusion
  (73 shorter events, 11.4 us)
Async XLA Ops:
  7.2 160.1 %all-gather.7.cloned.1.call-start = ((), (), s32[]{:S(2)}) async-start(), calls=%async_computation.2 | async-start | bytes 7077888 | tf_op jit(solution)/shard_map/all_gather | solution.py:43
  11.6 102.1 %copy-start.3 = (bf16[3,3072,128]{2,1,0:T(8,128)(2,1)}, bf16[3,3072,128]{2,1,0:T(8,128)(2,1)S(1)}, u32[]{:S(2)}) copy-start(bf16[3,3072,128]{2,1,0:T(8,128)(2,1)S(1)} %broadcast_multiply_fusion) | copy-start | bytes 7077892
  111.7 106.1 %all-gather.11.cloned.1.call-start = ((), (), s32[]{:S(2)}) async-start(), calls=%async_computation.4 | async-start | bytes 7077888 | tf_op jit(solution)/shard_map/all_gather | solution.py:43
  112.4 165.6 %all-gather.9.cloned.1.call-start = ((), (), s32[]{:S(2)}) async-start(), calls=%async_computation.3 | async-start | bytes 7077888 | tf_op jit(solution)/shard_map/all_gather | solution.py:43
  112.5 53.7 %collective-permute-start.1 = (bf16[3,3072,128]{2,1,0:T(8,128)(2,1)S(1)}, bf16[3,3072,128]{2,1,0:T(8,128)(2,1)}, u32[]{:S(2)}, u32[]{:S(2)}) collective-permute-start(bf16[3,3072,128]{2,1,0:T(8,128)(2,1)S(1)} %broadcast_multiply_fusion), channel_id=1, source_target_pairs={{1,0},{2,1},{3,2},{5,4},{6,5},{7,6},{9,8},{10,9},{11,10},{13,12},{... | collective-permute-start | bytes 7077896 | tf_op jit(solution)/shard_map/ppermute | solution.py:41
  113.8 53.5 %collective-permute-start = (bf16[3,3072,128]{2,1,0:T(8,128)(2,1)S(1)}, bf16[3,3072,128]{2,1,0:T(8,128)(2,1)}, u32[]{:S(2)}, u32[]{:S(2)}) collective-permute-start(bf16[3,3072,128]{2,1,0:T(8,128)(2,1)S(1)} %broadcast_multiply_fusion), channel_id=1, source_target_pairs={{0,1},{1,2},{2,3},{4,5},{5,6},{6,7},{8,9},{9,10},{10,11},{12,13},{... | collective-permute-start | bytes 7077896 | tf_op jit(solution)/shard_map/ppermute | solution.py:38
  201.9 63.5 %copy-start = (bf16[512,3072]{1,0:T(8,128)(2,1)}, bf16[512,3072]{1,0:T(8,128)(2,1)S(1)}, u32[]{:S(2)}) copy-start(bf16[512,3072]{1,0:T(8,128)(2,1)S(1)} %convolution_convert_fusion.2) | copy-start | bytes 9437188
  203.3 55.9 %collective-permute-start.2 = (bf16[3072,128]{0,1:T(8,128)(2,1)}, bf16[3072,128]{0,1:T(8,128)(2,1)}, u32[]{:S(2)}, u32[]{:S(2)}) collective-permute-start(bf16[3072,128]{0,1:T(8,128)(2,1)} %get-tuple-element.50), channel_id=1, source_target_pairs={{0,1},{1,2},{2,3},{4,5},{5,6},{6,7},{8,9},{9,10},{10,11},{12,13},{... | collective-permute-start | bytes 2359304 | tf_op jit(solution)/shard_map/ppermute | solution.py:38
  208.7 56.7 %collective-permute-start.5 = (bf16[3072,128]{0,1:T(8,128)(2,1)}, bf16[3072,128]{0,1:T(8,128)(2,1)}, u32[]{:S(2)}, u32[]{:S(2)}) collective-permute-start(bf16[3072,128]{0,1:T(8,128)(2,1)} %get-tuple-element.51), channel_id=1, source_target_pairs={{1,0},{2,1},{3,2},{5,4},{6,5},{7,6},{9,8},{10,9},{11,10},{13,12},{... | collective-permute-start | bytes 2359304 | tf_op jit(solution)/shard_map/ppermute | solution.py:41
  209.9 66.6 %collective-permute-start.8 = (bf16[3,3072,128]{2,1,0:T(8,128)(2,1)}, bf16[3,3072,128]{2,1,0:T(8,128)(2,1)}, u32[]{:S(2)}, u32[]{:S(2)}) collective-permute-start(bf16[3,3072,128]{2,1,0:T(8,128)(2,1)} %collective-permute-done), channel_id=1, source_target_pairs={{0,1},{1,2},{2,3},{4,5},{5,6},{6,7},{8,9},{9,10},{10,11},{12,13},{... | collective-permute-start | bytes 7077896 | tf_op jit(solution)/shard_map/ppermute | solution.py:38
  216.0 65.8 %collective-permute-start.9 = (bf16[3,3072,128]{2,1,0:T(8,128)(2,1)}, bf16[3,3072,128]{2,1,0:T(8,128)(2,1)}, u32[]{:S(2)}, u32[]{:S(2)}) collective-permute-start(bf16[3,3072,128]{2,1,0:T(8,128)(2,1)} %collective-permute-done.1), channel_id=1, source_target_pairs={{1,0},{2,1},{3,2},{5,4},{6,5},{7,6},{9,8},{10,9},{11,10},{13,12},{... | collective-permute-start | bytes 7077896 | tf_op jit(solution)/shard_map/ppermute | solution.py:41
  257.9 60.7 %collective-permute-start.21 = (bf16[3072,128]{0,1:T(8,128)(2,1)}, bf16[3072,128]{0,1:T(8,128)(2,1)}, u32[]{:S(2)}, u32[]{:S(2)}) collective-permute-start(bf16[3072,128]{0,1:T(8,128)(2,1)} %get-tuple-element.59), channel_id=1, source_target_pairs={{1,0},{2,1},{3,2},{5,4},{6,5},{7,6},{9,8},{10,9},{11,10},{13,12},{... | collective-permute-start | bytes 2359304 | tf_op jit(solution)/shard_map/ppermute | solution.py:41
  259.2 61.0 %collective-permute-start.18 = (bf16[3072,128]{0,1:T(8,128)(2,1)}, bf16[3072,128]{0,1:T(8,128)(2,1)}, u32[]{:S(2)}, u32[]{:S(2)}) collective-permute-start(bf16[3072,128]{0,1:T(8,128)(2,1)} %get-tuple-element.60), channel_id=1, source_target_pairs={{0,1},{1,2},{2,3},{4,5},{5,6},{6,7},{8,9},{9,10},{10,11},{12,13},{... | collective-permute-start | bytes 2359304 | tf_op jit(solution)/shard_map/ppermute | solution.py:38
  268.4 58.3 %collective-permute-start.3 = (bf16[3072,128]{0,1:T(8,128)(2,1)}, bf16[3072,128]{0,1:T(8,128)(2,1)}, u32[]{:S(2)}, u32[]{:S(2)}) collective-permute-start(bf16[3072,128]{0,1:T(8,128)(2,1)} %get-tuple-element.48), channel_id=1, source_target_pairs={{0,1},{1,2},{2,3},{4,5},{5,6},{6,7},{8,9},{9,10},{10,11},{12,13},{... | collective-permute-start | bytes 2359304 | tf_op jit(solution)/shard_map/ppermute | solution.py:38
  276.5 51.5 %collective-permute-start.6 = (bf16[3072,128]{0,1:T(8,128)(2,1)}, bf16[3072,128]{0,1:T(8,128)(2,1)}, u32[]{:S(2)}, u32[]{:S(2)}) collective-permute-start(bf16[3072,128]{0,1:T(8,128)(2,1)} %get-tuple-element.49), channel_id=1, source_target_pairs={{1,0},{2,1},{3,2},{5,4},{6,5},{7,6},{9,8},{10,9},{11,10},{13,12},{... | collective-permute-start | bytes 2359304 | tf_op jit(solution)/shard_map/ppermute | solution.py:41
  316.4 3.8 copy-start.2
  316.6 19.9 %collective-permute-start.10 = (bf16[3072,128]{0,1:T(8,128)(2,1)S(1)}, bf16[3072,128]{0,1:T(8,128)(2,1)S(1)}, u32[]{:S(2)}, u32[]{:S(2)}) collective-permute-start(bf16[3072,128]{0,1:T(8,128)(2,1)S(1)} %get-tuple-element.56), channel_id=1, source_target_pairs={{0,1},{1,2},{2,3},{4,5},{5,6},{6,7},{8,9},{9,10},{10,11},{12,13},{... | collective-permute-start | bytes 2359304 | tf_op jit(solution)/shard_map/ppermute | solution.py:38
  318.6 9.4 %copy-start.1 = (bf16[512,3072]{1,0:T(8,128)(2,1)S(1)}, bf16[512,3072]{1,0:T(8,128)(2,1)}, u32[]{:S(2)}) copy-start(bf16[512,3072]{1,0:T(8,128)(2,1)} %copy-done) | copy-start | bytes 9437188
  318.6 22.6 %collective-permute-start.13 = (bf16[3072,128]{0,1:T(8,128)(2,1)S(1)}, bf16[3072,128]{0,1:T(8,128)(2,1)S(1)}, u32[]{:S(2)}, u32[]{:S(2)}) collective-permute-start(bf16[3072,128]{0,1:T(8,128)(2,1)S(1)} %get-tuple-element.57), channel_id=1, source_target_pairs={{1,0},{2,1},{3,2},{5,4},{6,5},{7,6},{9,8},{10,9},{11,10},{13,12},{... | collective-permute-start | bytes 2359304 | tf_op jit(solution)/shard_map/ppermute | solution.py:41
  322.1 31.2 %collective-permute-start.19 = (bf16[3072,128]{0,1:T(8,128)(2,1)S(1)}, bf16[3072,128]{0,1:T(8,128)(2,1)S(1)}, u32[]{:S(2)}, u32[]{:S(2)}) collective-permute-start(bf16[3072,128]{0,1:T(8,128)(2,1)S(1)} %get-tuple-element.63), channel_id=1, source_target_pairs={{0,1},{1,2},{2,3},{4,5},{5,6},{6,7},{8,9},{9,10},{10,11},{12,13},{... | collective-permute-start | bytes 2359304 | tf_op jit(solution)/shard_map/ppermute | solution.py:38
  326.7 31.3 %collective-permute-start.22 = (bf16[3072,128]{0,1:T(8,128)(2,1)S(1)}, bf16[3072,128]{0,1:T(8,128)(2,1)S(1)}, u32[]{:S(2)}, u32[]{:S(2)}) collective-permute-start(bf16[3072,128]{0,1:T(8,128)(2,1)S(1)} %get-tuple-element.64), channel_id=1, source_target_pairs={{1,0},{2,1},{3,2},{5,4},{6,5},{7,6},{9,8},{10,9},{11,10},{13,12},{... | collective-permute-start | bytes 2359304 | tf_op jit(solution)/shard_map/ppermute | solution.py:41
  330.0 40.2 %collective-permute-start.4 = (bf16[3072,128]{0,1:T(8,128)(2,1)S(1)}, bf16[3072,128]{0,1:T(8,128)(2,1)S(1)}, u32[]{:S(2)}, u32[]{:S(2)}) collective-permute-start(bf16[3072,128]{0,1:T(8,128)(2,1)S(1)} %get-tuple-element.46), channel_id=1, source_target_pairs={{0,1},{1,2},{2,3},{4,5},{5,6},{6,7},{8,9},{9,10},{10,11},{12,13},{... | collective-permute-start | bytes 2359304 | tf_op jit(solution)/shard_map/ppermute | solution.py:38
  336.5 38.4 %collective-permute-start.7 = (bf16[3072,128]{0,1:T(8,128)(2,1)S(1)}, bf16[3072,128]{0,1:T(8,128)(2,1)S(1)}, u32[]{:S(2)}, u32[]{:S(2)}) collective-permute-start(bf16[3072,128]{0,1:T(8,128)(2,1)S(1)} %get-tuple-element.47), channel_id=1, source_target_pairs={{1,0},{2,1},{3,2},{5,4},{6,5},{7,6},{9,8},{10,9},{11,10},{13,12},{... | collective-permute-start | bytes 2359304 | tf_op jit(solution)/shard_map/ppermute | solution.py:41
  341.2 103.8 %collective-permute-start.16 = (bf16[3,3072,128]{2,1,0:T(8,128)(2,1)}, bf16[3,3072,128]{2,1,0:T(8,128)(2,1)S(1)}, u32[]{:S(2)}, u32[]{:S(2)}) collective-permute-start(bf16[3,3072,128]{2,1,0:T(8,128)(2,1)} %collective-permute-done.8), channel_id=1, source_target_pairs={{0,1},{1,2},{2,3},{4,5},{5,6},{6,7},{8,9},{9,10},{10,11},{12,13},{... | collective-permute-start | bytes 7077896 | tf_op jit(solution)/shard_map/ppermute | solution.py:38
  353.3 93.2 %collective-permute-start.17 = (bf16[3,3072,128]{2,1,0:T(8,128)(2,1)}, bf16[3,3072,128]{2,1,0:T(8,128)(2,1)S(1)}, u32[]{:S(2)}, u32[]{:S(2)}) collective-permute-start(bf16[3,3072,128]{2,1,0:T(8,128)(2,1)} %collective-permute-done.9), channel_id=1, source_target_pairs={{1,0},{2,1},{3,2},{5,4},{6,5},{7,6},{9,8},{10,9},{11,10},{13,12},{... | collective-permute-start | bytes 7077896 | tf_op jit(solution)/shard_map/ppermute | solution.py:41
  358.1 79.5 %collective-permute-start.11 = (bf16[3072,128]{0,1:T(8,128)(2,1)S(1)}, bf16[3072,128]{0,1:T(8,128)(2,1)S(1)}, u32[]{:S(2)}, u32[]{:S(2)}) collective-permute-start(bf16[3072,128]{0,1:T(8,128)(2,1)S(1)} %get-tuple-element.54), channel_id=1, source_target_pairs={{0,1},{1,2},{2,3},{4,5},{5,6},{6,7},{8,9},{9,10},{10,11},{12,13},{... | collective-permute-start | bytes 2359304 | tf_op jit(solution)/shard_map/ppermute | solution.py:38
  362.5 76.4 %copy-start.4 = (bf16[3,3072,128]{2,1,0:T(8,128)(2,1)S(1)}, bf16[3,3072,128]{2,1,0:T(8,128)(2,1)}, u32[]{:S(2)}) copy-start(bf16[3,3072,128]{2,1,0:T(8,128)(2,1)} %copy-done.3) | copy-start | bytes 7077892
  370.2 84.3 %collective-permute-start.20 = (bf16[3072,128]{0,1:T(8,128)(2,1)S(1)}, bf16[3072,128]{0,1:T(8,128)(2,1)S(1)}, u32[]{:S(2)}, u32[]{:S(2)}) collective-permute-start(bf16[3072,128]{0,1:T(8,128)(2,1)S(1)} %get-tuple-element.61), channel_id=1, source_target_pairs={{0,1},{1,2},{2,3},{4,5},{5,6},{6,7},{8,9},{9,10},{10,11},{12,13},{... | collective-permute-start | bytes 2359304 | tf_op jit(solution)/shard_map/ppermute | solution.py:38
  374.9 66.2 %collective-permute-start.14 = (bf16[3072,128]{0,1:T(8,128)(2,1)S(1)}, bf16[3072,128]{0,1:T(8,128)(2,1)S(1)}, u32[]{:S(2)}, u32[]{:S(2)}) collective-permute-start(bf16[3072,128]{0,1:T(8,128)(2,1)S(1)} %get-tuple-element.55), channel_id=1, source_target_pairs={{1,0},{2,1},{3,2},{5,4},{6,5},{7,6},{9,8},{10,9},{11,10},{13,12},{... | collective-permute-start | bytes 2359304 | tf_op jit(solution)/shard_map/ppermute | solution.py:41
  437.6 22.8 %collective-permute-start.23 = (bf16[3072,128]{0,1:T(8,128)(2,1)S(1)}, bf16[3072,128]{0,1:T(8,128)(2,1)S(1)}, u32[]{:S(2)}, u32[]{:S(2)}) collective-permute-start(bf16[3072,128]{0,1:T(8,128)(2,1)S(1)} %get-tuple-element.62), channel_id=1, source_target_pairs={{1,0},{2,1},{3,2},{5,4},{6,5},{7,6},{9,8},{10,9},{11,10},{13,12},{... | collective-permute-start | bytes 2359304 | tf_op jit(solution)/shard_map/ppermute | solution.py:41
  439.3 21.0 %copy-start.5 = (bf16[3072,128]{0,1:T(8,128)(2,1)S(1)}, bf16[3072,128]{0,1:T(8,128)(2,1)}, u32[]{:S(2)}) copy-start(bf16[3072,128]{0,1:T(8,128)(2,1)} %get-tuple-element.25) | copy-start | bytes 2359300
  439.3 21.0 %copy-start.8 = (f32[1,3072]{1,0:T(1,128)S(1)}, f32[1,3072]{1,0:T(1,128)}, u32[]{:S(2)}) copy-start(f32[1,3072]{1,0:T(1,128)} %get-tuple-element.75) | copy-start | bytes 36868
  441.7 29.6 %collective-permute-start.12 = (bf16[3072,128]{0,1:T(8,128)(2,1)S(1)}, bf16[3072,128]{0,1:T(8,128)(2,1)S(1)}, u32[]{:S(2)}, u32[]{:S(2)}) collective-permute-start(bf16[3072,128]{0,1:T(8,128)(2,1)S(1)} %get-tuple-element.52), channel_id=1, source_target_pairs={{0,1},{1,2},{2,3},{4,5},{5,6},{6,7},{8,9},{9,10},{10,11},{12,13},{... | collective-permute-start | bytes 2359304 | tf_op jit(solution)/shard_map/ppermute | solution.py:38
  445.0 26.4 %collective-permute-start.15 = (bf16[3072,128]{0,1:T(8,128)(2,1)S(1)}, bf16[3072,128]{0,1:T(8,128)(2,1)S(1)}, u32[]{:S(2)}, u32[]{:S(2)}) collective-permute-start(bf16[3072,128]{0,1:T(8,128)(2,1)S(1)} %get-tuple-element.53), channel_id=1, source_target_pairs={{1,0},{2,1},{3,2},{5,4},{6,5},{7,6},{9,8},{10,9},{11,10},{13,12},{... | collective-permute-start | bytes 2359304 | tf_op jit(solution)/shard_map/ppermute | solution.py:41
  470.1 1.3 copy-start.7
  473.8 1.8 collective-permute-start.24
  475.7 11.2 %collective-permute-start.25 = (bf16[3,512,128]{2,1,0:T(8,128)(2,1)S(1)}, bf16[3,512,128]{2,1,0:T(8,128)(2,1)S(1)}, u32[]{:S(2)}, u32[]{:S(2)}) collective-permute-start(bf16[3,512,128]{2,1,0:T(8,128)(2,1)S(1)} %add_convert_fusion.1), channel_id=1, source_target_pairs={{0,8},{4,12},{8,0},{12,4},{16,24},{20,28},{24,16},{28,20},{1,9},{5... | collective-permute-start | bytes 1179656 | tf_op jit(solution)/shard_map/ppermute | solution.py:94
  487.1 10.5 %collective-permute-start.26 = (bf16[3,512,128]{2,1,0:T(8,128)(2,1)S(1)}, bf16[3,512,128]{2,1,0:T(8,128)(2,1)}, u32[]{:S(2)}, u32[]{:S(2)}) collective-permute-start(bf16[3,512,128]{2,1,0:T(8,128)(2,1)S(1)} %add_convert_fusion), channel_id=1, source_target_pairs={{0,16},{4,20},{8,24},{12,28},{16,0},{20,4},{24,8},{28,12},{1,17},{... | collective-permute-start | bytes 1179656 | tf_op jit(solution)/shard_map/ppermute | solution.py:94
  488.0 9.6 %copy-start.6 = (f32[3,512,128]{2,1,0:T(8,128)S(1)}, f32[3,512,128]{2,1,0:T(8,128)}, u32[]{:S(2)}) copy-start(f32[3,512,128]{2,1,0:T(8,128)} %param.7) | copy-start | bytes 2359300
Sparse Core Ops, SparseCore 0:
  111.8 44.5 all-gather.6
  158.2 46.5 all-gather.10
  207.3 46.5 all-gather.8
where the time goes:
time: 514 us; the launch traced here: 506 us
  waiting for transfers between devices  175 us (34%)
  blocking collectives  92.4 us (18%)
  matrix products  85 us (17%)
  starting transfers between devices  73.1 us (14%)
  local copies, waits for them, and re-layouts  41.9 us (8%)
  other arithmetic  24.3 us (5%)
  between operations  14.7 us (3%)
    ppermute x12, waiting for transfers between devices, up(): return lax.ppermute(value, 'col', up_moves)  91.1 us
    dot_general x3, matrix products, on_device(): jnp.dot(resident_inverse, blocks, preferred_element_type=jnp.float32)  80.1 us
    ppermute x12, waiting for transfers between devices, down(): return lax.ppermute(value, 'col', down_moves)  64.3 us
    all_to_all x1, blocking collectives, on_device(): spread = lax.all_to_all(spread, 'col', 0, 0, tiled=True)  58 us
    ppermute x12, starting transfers between devices, up(): return lax.ppermute(value, 'col', up_moves)  54.3 us
    all_to_all x1, blocking collectives, on_device(): spread = lax.all_to_all(spread, 'row', 0, 0, tiled=True)  34.4 us
    ppermute x3, waiting for transfers between devices, on_device(): got = lax.ppermute(sent, 'row', [(i, i ^ step) for i in range(row_count)])  18.6 us
    optimization_barrier x2, local copies, waits for them, and re-layouts, on_device(): lax.optimization_barrier((gathered[by - 1], low, high))  17.5 us
  transfers between devices with their start and end apart: 30, of which 17 were waited for; matrix products, arithmetic and copies ran while one was open for 27% of the time, Pallas kernels for 0%

commit v1 on v0

v1 whole, which is shorter than its diff:
```python
import jax
import jax.numpy as jnp
from jax import lax
from jax.sharding import PartitionSpec as P


def slot_rows(anc_tiles, slot_tile, tile_rows):
    listed = (anc_tiles[:, :, None] == slot_tile[None, None, :]).any(axis=1)
    return jnp.repeat(listed.astype(jnp.float32), tile_rows, axis=1)


def on_device(resident_inverse, factor, diag_inverse, anc_tiles, slot_tile):
    own_rows, own_cols = resident_inverse.shape
    supers, _, part_width = factor.shape
    row_index = lax.axis_index("row")
    col_index = lax.axis_index("col")
    col_count = lax.axis_size("col")
    row_count = lax.axis_size("row")
    ratio = row_count // col_count
    owners = row_count // ratio
    total_rows = own_rows * row_count
    row_mask = slot_rows(anc_tiles, slot_tile, total_rows // slot_tile.shape[0])
    own_mask = lax.dynamic_slice_in_dim(row_mask, row_index * own_rows, own_rows, 1)
    mine = [factor[s] * own_mask[s].astype(jnp.bfloat16)[:, None] for s in range(supers)]
    last = col_count - 1
    up_moves = [(i, i + 1) for i in range(last)]
    down_moves = [(i + 1, i) for i in range(last)]
    chunk = own_cols // row_count

    parts = []
    for s in range(supers):
        ups, downs = [mine[s]], [mine[s]]
        for by in range(last):
            ups.append(lax.ppermute(ups[-1], "col", up_moves))
            downs.append(lax.ppermute(downs[-1], "col", down_moves))
        parts.append([mine[s]] + [ups[by] + downs[col_count - by] for by in range(1, col_count)])

    news, contribs = [], []
    for s in range(supers):
        wide = jnp.concatenate(parts[s], axis=1)
        partial = lax.dot_general(
            resident_inverse, wide, (((0,), (0,)), ((), ())), preferred_element_type=jnp.float32
        ).astype(jnp.bfloat16)
        summed = lax.psum_scatter(partial, "row", scatter_dimension=0, tiled=True)
        got = [summed[:, :part_width]]
        for by in range(1, col_count):
            piece = summed[:, by * part_width:(by + 1) * part_width]
            got.append(lax.ppermute(piece, "col", [(c, (c - by) % col_count) for c in range(col_count)]))
        got = jnp.stack(got)
        home = []
        for k in range(owners):
            block = (row_index + k) % owners
            piece = lax.dynamic_index_in_dim(got, (block - col_index) % col_count, 0, keepdims=False)
            moves = [(r, ratio * ((r + k) % owners) + r // owners) for r in range(row_count)]
            home.append(lax.ppermute(piece, "row", moves))
        home = jnp.stack(home)
        mine_y = jnp.concatenate([
            lax.dynamic_index_in_dim(home, (row_index // ratio - q) % owners, 0, keepdims=False)
            for q in range(owners)
        ], axis=0)
        news.append(-(mine_y * own_mask[s].astype(jnp.bfloat16)[:, None]))
        contribs.append(jnp.stack([
            jnp.einsum("rw,rv->wv", part, mine_y, preferred_element_type=jnp.float32)
            for part in parts[s]
        ]))
    stacked = jnp.stack(contribs, axis=1)
    ordered = jnp.stack([
        lax.dynamic_index_in_dim(stacked, (col_index - q) % col_count, 0, keepdims=False)
        for q in range(col_count)
    ], axis=1)
    totals = ordered.reshape(supers, col_count * part_width, part_width)
    step = 1
    while step < row_count:
        sent = totals.astype(jnp.bfloat16)
        got = lax.ppermute(sent, "row", [(i, i ^ step) for i in range(row_count)])
        totals = sent.astype(jnp.float32) + got.astype(jnp.float32)
        step *= 2
    return (jnp.stack(news), diag_inverse + totals)


def solution(mesh):
    placed = (P("row", "col"), P(None, "row", "col"), P(None, None, "col"), P(), P())
    return jax.shard_map(
        on_device,
        mesh=mesh,
        in_specs=placed,
        out_specs=(P(None, "row", "col"), P(None, None, "col")),
        check_vma=False,
    )
```

time: 514 us -> 440 us (0.86)
  blocking collectives: 92.4 us -> 0 us
  starting transfers between devices: 73.1 us -> 101 us
  local copies, waits for them, and re-layouts: 41.9 us -> 24.4 us
  waiting for transfers between devices: 175 us -> 190 us
  other arithmetic: 24.3 us -> 17.2 us
    all_to_all x2 -> x0, blocking collectives: 92.4 us -> none  [the longest x1 58 us: on_device(): spread = lax.all_to_all(spread, 'col', 0, 0, tiled=True)]
    reduce_scatter x0 -> x3, waiting for transfers between devices: none -> 49 us  [on_device(): summed = lax.psum_scatter(partial, 'row', scatter_dimension=0, tiled=True)]
    ppermute x24 -> x39, waiting for transfers between devices: 155 us -> 122 us  [the longest x9 112 us: on_device(): downs.append(lax.ppermute(downs[-1], 'col', down_moves))]
    ppermute x24 -> x39, starting transfers between devices: 70.8 us -> 99.3 us  [the longest x9 44 us: on_device(): ups.append(lax.ppermute(ups[-1], 'col', up_moves))]
    optimization_barrier x2 -> x0, local copies, waits for them, and re-layouts: 17.5 us -> none  [on_device(): lax.optimization_barrier((gathered[by - 1], low, high))]
    add x6 -> x0, other arithmetic: 8.66 us -> none  [on_device(): from_below = from_below + piece(s, col_index + by - 1)]
    all_gather x1 -> x0, local copies, waits for them, and re-layouts: 8.65 us -> none  [on_device(): lax.all_gather(spread[s], 'row', axis=1, tiled=True)]
    another operation x0 -> x4, local copies, waits for them, and re-layouts: none -> 6.4 us  [the longest x3 6.38 us: on_device(): got = jnp.stack(got)]
  transfers between devices with their start and end apart: 30 -> 45, of which waited for: 17 -> 17; matrix products, arithmetic and copies ran while one was open for 27% -> 19% of each run, Pallas kernels for 0% -> 0%
where the time goes in v1:
time: 440 us; the launch traced here: 431 us
  waiting for transfers between devices  190 us (43%)
  starting transfers between devices  101 us (23%)
  matrix products  83.7 us (19%)
  local copies, waits for them, and re-layouts  24.4 us (6%)
  other arithmetic  17.2 us (4%)
  between operations  15.1 us (3%)
    ppermute x9, waiting for transfers between devices, on_device(): downs.append(lax.ppermute(downs[-1], 'col', down_moves))  112 us
    dot_general x3, matrix products, on_device(): lax.dot_general(resident_inverse, wide, (((0,), (0,)), ((), ())), preferr...  78.8 us
    reduce_scatter x3, waiting for transfers between devices, on_device(): summed = lax.psum_scatter(partial, 'row', scatter_dimension=0, tiled=True)  49 us
    ppermute x9, starting transfers between devices, on_device(): ups.append(lax.ppermute(ups[-1], 'col', up_moves))  44 us
    ppermute x12, starting transfers between devices, on_device(): home.append(lax.ppermute(piece, 'row', moves))  28.8 us
    ppermute x3, waiting for transfers between devices, on_device(): got = lax.ppermute(sent, 'row', [(i, i ^ step) for i in range(row_count)])  19.6 us
    ppermute x9, starting transfers between devices, on_device(): lax.ppermute(piece, 'col', [(c, (c - by) % col_count) for c in range(col_...  14.9 us
    ppermute x9, starting transfers between devices, on_device(): downs.append(lax.ppermute(downs[-1], 'col', down_moves))  11.6 us
  transfers between devices with their start and end apart: 45, of which 17 were waited for; matrix products, arithmetic and copies ran while one was open for 19% of the time, Pallas kernels for 0%

profile of v1, /device:TPU:0, one launch (start us, length us, event | category | flops | bytes accessed | tf_op | source)
XLA Modules:
  0.0 431.2 jit_solution(9820188700037462310)
XLA Ops:
  8.4 3.9 bitcast_multiply_fusion.2
  12.4 1.3 collective-permute-start.1
  13.7 5.6 %collective-permute-start = (bf16[3072,128]{1,0:T(8,128)(2,1)S(1)}, bf16[3072,128]{1,0:T(8,128)(2,1)S(1)}, u32[]{:S(2)}, u32[]{:S(2)}) collective-permute-start(bf16[3072,128]{1,0:T(8,128)(2,1)S(1)} %get-tuple-element.5), channel_id=1, source_target_pairs={{0,1},{1,2},{2,3},{4,5},{5,6},{6,7},{8,9},{9,10},{10,11},{12,13},{... | collective-permute-start | bytes 2359304 | tf_op jit(solution)/shard_map/ppermute | solution.py:34
  19.3 15.6 %collective-permute-done.1 = bf16[3072,128]{1,0:T(8,128)(2,1)S(1)} collective-permute-done((bf16[3072,128]{1,0:T(8,128)(2,1)S(1)}, bf16[3072,128]{1,0:T(8,128)(2,1)S(1)}, u32[]{:S(2)}, u32[]{:S(2)}) %collective-permute-start.1) | collective-permute-done | bytes 786464 | tf_op jit(solution)/shard_map/ppermute | solution.py:35
  34.9 1.3 collective-permute-start.2
  36.2 4.6 %collective-permute-start.4 = (bf16[3072,128]{1,0:T(8,128)(2,1)S(1)}, bf16[3072,128]{1,0:T(8,128)(2,1)S(1)}, u32[]{:S(2)}, u32[]{:S(2)}) collective-permute-start(bf16[3072,128]{1,0:T(8,128)(2,1)S(1)} %collective-permute-done), channel_id=1, source_target_pairs={{0,1},{1,2},{2,3},{4,5},{5,6},{6,7},{8,9},{9,10},{10,11},{12,13},{... | collective-permute-start | bytes 2359304 | tf_op jit(solution)/shard_map/ppermute | solution.py:34
  40.8 14.7 %collective-permute-done.2 = bf16[3072,128]{1,0:T(8,128)(2,1)S(1)} collective-permute-done((bf16[3072,128]{1,0:T(8,128)(2,1)S(1)}, bf16[3072,128]{1,0:T(8,128)(2,1)S(1)}, u32[]{:S(2)}, u32[]{:S(2)}) %collective-permute-start.2) | collective-permute-done | bytes 786464 | tf_op jit(solution)/shard_map/ppermute | solution.py:35
  55.5 1.3 collective-permute-start.3
  56.8 4.6 %collective-permute-start.5 = (bf16[3072,128]{1,0:T(8,128)(2,1)S(1)}, bf16[3072,128]{1,0:T(8,128)(2,1)S(1)}, u32[]{:S(2)}, u32[]{:S(2)}) collective-permute-start(bf16[3072,128]{1,0:T(8,128)(2,1)S(1)} %collective-permute-done.4), channel_id=1, source_target_pairs={{0,1},{1,2},{2,3},{4,5},{5,6},{6,7},{8,9},{9,10},{10,11},{12,13},{... | collective-permute-start | bytes 2359304 | tf_op jit(solution)/shard_map/ppermute | solution.py:34
  61.6 13.6 %collective-permute-done.3 = bf16[3072,128]{1,0:T(8,128)(2,1)S(1)} collective-permute-done((bf16[3072,128]{1,0:T(8,128)(2,1)S(1)}, bf16[3072,128]{1,0:T(8,128)(2,1)S(1)}, u32[]{:S(2)}, u32[]{:S(2)}) %collective-permute-start.3) | collective-permute-done | bytes 786464 | tf_op jit(solution)/shard_map/ppermute | solution.py:35
  76.6 26.2 %fusion = bf16[6144,512]{0,1:T(8,128)(2,1)} fusion(bf16[3072,6144]{1,0:T(8,128)(2,1)} %param.5, bf16[3072,128]{1,0:T(8,128)(2,1)S(1)} %add.200, bf16[3072,128]{1,0:T(8,128)(2,1)S(1)} %add.199, bf16[3072,128]{1,0:T(8,128)(2,1)S(1)} %add.198, bf16[3072,128]{1,0:T(8,128)(2,1)S(1)} %get-tuple-element.5), kind=kOutput, calls=%fused_computation.3 | convolution fusion | flops 19343081472 | bytes 47185920 | tf_op jit(solution)/shard_map/dot_general | solution.py:41
  102.9 1.3 collective-permute-start.14
  104.2 5.1 %collective-permute-start.13 = (bf16[3072,128]{1,0:T(8,128)(2,1)}, bf16[3072,128]{1,0:T(8,128)(2,1)S(1)}, u32[]{:S(2)}, u32[]{:S(2)}) collective-permute-start(bf16[3072,128]{1,0:T(8,128)(2,1)} %get-tuple-element.7), channel_id=1, source_target_pairs={{0,1},{1,2},{2,3},{4,5},{5,6},{6,7},{8,9},{9,10},{10,11},{12,13},{... | collective-permute-start | bytes 2359304 | tf_op jit(solution)/shard_map/ppermute | solution.py:34
  109.3 13.2 %collective-permute-done.14 = bf16[3072,128]{1,0:T(8,128)(2,1)S(1)} collective-permute-done((bf16[3072,128]{1,0:T(8,128)(2,1)}, bf16[3072,128]{1,0:T(8,128)(2,1)S(1)}, u32[]{:S(2)}, u32[]{:S(2)}) %collective-permute-start.14) | collective-permute-done | bytes 786464 | tf_op jit(solution)/shard_map/ppermute | solution.py:35
  122.5 1.3 collective-permute-start.15
  123.8 4.6 %collective-permute-start.17 = (bf16[3072,128]{1,0:T(8,128)(2,1)S(1)}, bf16[3072,128]{1,0:T(8,128)(2,1)S(1)}, u32[]{:S(2)}, u32[]{:S(2)}) collective-permute-start(bf16[3072,128]{1,0:T(8,128)(2,1)S(1)} %collective-permute-done.13), channel_id=1, source_target_pairs={{0,1},{1,2},{2,3},{4,5},{5,6},{6,7},{8,9},{9,10},{10,11},{12,13},{... | collective-permute-start | bytes 2359304 | tf_op jit(solution)/shard_map/ppermute | solution.py:34
  128.4 12.1 %collective-permute-done.15 = bf16[3072,128]{1,0:T(8,128)(2,1)S(1)} collective-permute-done((bf16[3072,128]{1,0:T(8,128)(2,1)S(1)}, bf16[3072,128]{1,0:T(8,128)(2,1)S(1)}, u32[]{:S(2)}, u32[]{:S(2)}) %collective-permute-start.15) | collective-permute-done | bytes 786464 | tf_op jit(solution)/shard_map/ppermute | solution.py:35
  140.5 1.3 collective-permute-start.16
  141.8 5.1 %collective-permute-start.18 = (bf16[3072,128]{1,0:T(8,128)(2,1)S(1)}, bf16[3072,128]{1,0:T(8,128)(2,1)S(1)}, u32[]{:S(2)}, u32[]{:S(2)}) collective-permute-start(bf16[3072,128]{1,0:T(8,128)(2,1)S(1)} %collective-permute-done.17), channel_id=1, source_target_pairs={{0,1},{1,2},{2,3},{4,5},{5,6},{6,7},{8,9},{9,10},{10,11},{12,13},{... | collective-permute-start | bytes 2359304 | tf_op jit(solution)/shard_map/ppermute | solution.py:34
  147.1 10.7 %collective-permute-done.16 = bf16[3072,128]{1,0:T(8,128)(2,1)S(1)} collective-permute-done((bf16[3072,128]{1,0:T(8,128)(2,1)S(1)}, bf16[3072,128]{1,0:T(8,128)(2,1)S(1)}, u32[]{:S(2)}, u32[]{:S(2)}) %collective-permute-start.16) | collective-permute-done | bytes 786464 | tf_op jit(solution)/shard_map/ppermute | solution.py:35
  160.1 26.3 %fusion.1 = bf16[6144,512]{0,1:T(8,128)(2,1)} fusion(bf16[3072,6144]{1,0:T(8,128)(2,1)} %param.5, bf16[3072,128]{1,0:T(8,128)(2,1)S(1)} %add.226, bf16[3072,128]{1,0:T(8,128)(2,1)S(1)} %add.225, bf16[3072,128]{1,0:T(8,128)(2,1)S(1)} %add.224, bf16[3072,128]{1,0:T(8,128)(2,1)S(1)} %copy-done.15), kind=kOutput, calls=%fused_computation.4 | convolution fusion | flops 19343081472 | bytes 47185920 | tf_op jit(solution)/shard_map/dot_general | solution.py:41
  186.5 1.3 collective-permute-start.27
  187.8 5.1 %collective-permute-start.26 = (bf16[3072,128]{1,0:T(8,128)(2,1)S(1)}, bf16[3072,128]{1,0:T(8,128)(2,1)S(1)}, u32[]{:S(2)}, u32[]{:S(2)}) collective-permute-start(bf16[3072,128]{1,0:T(8,128)(2,1)S(1)} %get-tuple-element.6), channel_id=1, source_target_pairs={{0,1},{1,2},{2,3},{4,5},{5,6},{6,7},{8,9},{9,10},{10,11},{12,13},{... | collective-permute-start | bytes 2359304 | tf_op jit(solution)/shard_map/ppermute | solution.py:34
  192.9 11.8 %collective-permute-done.27 = bf16[3072,128]{1,0:T(8,128)(2,1)S(1)} collective-permute-done((bf16[3072,128]{1,0:T(8,128)(2,1)S(1)}, bf16[3072,128]{1,0:T(8,128)(2,1)S(1)}, u32[]{:S(2)}, u32[]{:S(2)}) %collective-permute-start.27) | collective-permute-done | bytes 786464 | tf_op jit(solution)/shard_map/ppermute | solution.py:35
  204.8 1.3 collective-permute-start.28
  206.1 4.6 %collective-permute-start.30 = (bf16[3072,128]{1,0:T(8,128)(2,1)S(1)}, bf16[3072,128]{1,0:T(8,128)(2,1)S(1)}, u32[]{:S(2)}, u32[]{:S(2)}) collective-permute-start(bf16[3072,128]{1,0:T(8,128)(2,1)S(1)} %collective-permute-done.26), channel_id=1, source_target_pairs={{0,1},{1,2},{2,3},{4,5},{5,6},{6,7},{8,9},{9,10},{10,11},{12,13},{... | collective-permute-start | bytes 2359304 | tf_op jit(solution)/shard_map/ppermute | solution.py:34
  210.7 11.8 %collective-permute-done.28 = bf16[3072,128]{1,0:T(8,128)(2,1)S(1)} collective-permute-done((bf16[3072,128]{1,0:T(8,128)(2,1)S(1)}, bf16[3072,128]{1,0:T(8,128)(2,1)S(1)}, u32[]{:S(2)}, u32[]{:S(2)}) %collective-permute-start.28) | collective-permute-done | bytes 786464 | tf_op jit(solution)/shard_map/ppermute | solution.py:35
  222.5 1.3 collective-permute-start.29
  223.8 4.8 %collective-permute-start.31 = (bf16[3072,128]{1,0:T(8,128)(2,1)S(1)}, bf16[3072,128]{1,0:T(8,128)(2,1)S(1)}, u32[]{:S(2)}, u32[]{:S(2)}) collective-permute-start(bf16[3072,128]{1,0:T(8,128)(2,1)S(1)} %collective-permute-done.30), channel_id=1, source_target_pairs={{0,1},{1,2},{2,3},{4,5},{5,6},{6,7},{8,9},{9,10},{10,11},{12,13},{... | collective-permute-start | bytes 2359304 | tf_op jit(solution)/shard_map/ppermute | solution.py:34
  228.8 8.3 %collective-permute-done.29 = bf16[3072,128]{1,0:T(8,128)(2,1)S(1)} collective-permute-done((bf16[3072,128]{1,0:T(8,128)(2,1)S(1)}, bf16[3072,128]{1,0:T(8,128)(2,1)S(1)}, u32[]{:S(2)}, u32[]{:S(2)}) %collective-permute-start.29) | collective-permute-done | bytes 786464 | tf_op jit(solution)/shard_map/ppermute | solution.py:35
  239.4 26.3 %fusion.2 = bf16[6144,512]{0,1:T(8,128)(2,1)} fusion(bf16[3072,6144]{1,0:T(8,128)(2,1)} %param.5, bf16[3072,128]{1,0:T(8,128)(2,1)S(1)} %add.229, bf16[3072,128]{1,0:T(8,128)(2,1)S(1)} %add.228, bf16[3072,128]{1,0:T(8,128)(2,1)S(1)} %add.227, bf16[3072,128]{1,0:T(8,128)(2,1)S(1)} %get-tuple-element.6), kind=kOutput, calls=%fused_computation.5 | convolution fusion | flops 19343081472 | bytes 47185920 | tf_op jit(solution)/shard_map/dot_general | solution.py:41
  266.0 2.1 slice_bitcast_fusion.2
  268.1 4.1 collective-permute-start.6
  272.2 1.6 collective-permute-start.8
  273.8 2.2 slice_bitcast_fusion.1
  276.0 2.1 collective-permute-start.19
  278.1 1.2 collective-permute-start.20
  279.3 48.9 %reduce-scatter.8.cloned.1.call-done = bf16[768,512]{0,1:T(8,128)(2,1)} async-done(((bf16[6144,512]{0,1:T(8,128)(2,1)}), bf16[768,512]{0,1:T(8,128)(2,1)}) %reduce-scatter.8.cloned.1.call-update) | async-done | bytes 786448 | tf_op jit(solution)/shard_map/reduce_scatter | solution.py:44
  328.3 2.1 slice_bitcast_fusion
  330.3 1.5 collective-permute-start.21
  331.8 2.3 collective-permute-start.32
  334.8 1.0 pad_maximum_fusion.1
  336.5 1.5 collective-permute-start.34
  341.3 1.5 collective-permute-start.11
  342.8 1.9 collective-permute-start.12
  344.7 1.2 pad_maximum_fusion.3
  345.9 3.0 collective-permute-start.9
  348.9 6.9 %collective-permute-done.33 = bf16[768,128]{0,1:T(8,128)(2,1)} collective-permute-done((bf16[768,128]{0,1:T(8,128)(2,1)}, bf16[768,128]{0,1:T(8,128)(2,1)}, u32[]{:S(2)}, u32[]{:S(2)}) %collective-permute-start.33) | collective-permute-done | bytes 196640 | tf_op jit(solution)/shard_map/ppermute | solution.py:48
  355.8 3.4 collective-permute-start.10
  359.2 1.2 pad_maximum_fusion.5
  361.3 1.7 copy.30
  363.0 3.0 collective-permute-start.22
  366.0 1.8 copy.31
  369.4 3.4 collective-permute-start.23
  372.9 3.7 collective-permute-start.25
  377.5 1.4 pad_maximum_fusion.2
  380.7 4.8 %collective-permute-start.36 = (bf16[768,128]{1,0:T(8,128)(2,1)S(1)}, bf16[768,128]{1,0:T(8,128)(2,1)S(1)}, u32[]{:S(2)}, u32[]{:S(2)}) collective-permute-start(bf16[768,128]{1,0:T(8,128)(2,1)S(1)} %bitcast.195), channel_id=1, source_target_pairs={{0,8},{4,16},{8,24},{12,0},{16,12},{20,20},{24,28},{28,4},{1,9},{5... | collective-permute-start | bytes 589832 | tf_op jit(solution)/shard_map/ppermute | solution.py:55
  385.6 3.1 collective-permute-start.38
  388.8 1.1 pad_maximum_fusion.4
  400.4 1.2 collective-permute-done.39
  402.3 10.6 %collective-permute-done.40 = bf16[3,512,128]{2,1,0:T(8,128)(2,1)S(1)} collective-permute-done((bf16[3,512,128]{2,1,0:T(8,128)(2,1)S(1)}, bf16[3,512,128]{2,1,0:T(8,128)(2,1)S(1)}, u32[]{:S(2)}, u32[]{:S(2)}) %collective-permute-start.40) | collective-permute-done | bytes 393248 | tf_op jit(solution)/shard_map/ppermute | solution.py:75
  414.1 1.7 pad_maximum_fusion
  415.7 7.7 %collective-permute-done.41 = bf16[3,512,128]{2,1,0:T(8,128)(2,1)S(1)} collective-permute-done((bf16[3,512,128]{2,1,0:T(8,128)(2,1)S(1)}, bf16[3,512,128]{2,1,0:T(8,128)(2,1)S(1)}, u32[]{:S(2)}, u32[]{:S(2)}) %collective-permute-start.41) | collective-permute-done | bytes 393248 | tf_op jit(solution)/shard_map/ppermute | solution.py:75
  423.5 1.0 add_add_fusion
  (144 shorter events, 30.1 us)
Async XLA Ops:
  7.2 258.9 %reduce-scatter.4.cloned.1.call-start = ((), (), s32[]{:S(2)}) async-start(), calls=%async_computation.3 | async-start | bytes 7077888 | tf_op jit(solution)/shard_map/reduce_scatter | solution.py:44
  8.4 4.0 copy-start.20
  12.4 64.2 %copy-start.17 = (bf16[3072,128]{1,0:T(8,128)(2,1)}, bf16[3072,128]{1,0:T(8,128)(2,1)S(1)}, u32[]{:S(2)}) copy-start(bf16[3072,128]{1,0:T(8,128)(2,1)S(1)} %get-tuple-element.5) | copy-start | bytes 2359300
  12.4 226.1 %copy-start.13 = (bf16[3072,128]{1,0:T(8,128)(2,1)}, bf16[3072,128]{1,0:T(8,128)(2,1)S(1)}, u32[]{:S(2)}) copy-start(bf16[3072,128]{1,0:T(8,128)(2,1)S(1)} %get-tuple-element.6) | copy-start | bytes 2359300
  12.4 22.5 %collective-permute-start.1 = (bf16[3072,128]{1,0:T(8,128)(2,1)S(1)}, bf16[3072,128]{1,0:T(8,128)(2,1)S(1)}, u32[]{:S(2)}, u32[]{:S(2)}) collective-permute-start(bf16[3072,128]{1,0:T(8,128)(2,1)S(1)} %get-tuple-element.5), channel_id=1, source_target_pairs={{1,0},{2,1},{3,2},{5,4},{6,5},{7,6},{9,8},{10,9},{11,10},{13,12},{... | collective-permute-start | bytes 2359304 | tf_op jit(solution)/shard_map/ppermute | solution.py:35
  13.7 22.5 %collective-permute-start = (bf16[3072,128]{1,0:T(8,128)(2,1)S(1)}, bf16[3072,128]{1,0:T(8,128)(2,1)S(1)}, u32[]{:S(2)}, u32[]{:S(2)}) collective-permute-start(bf16[3072,128]{1,0:T(8,128)(2,1)S(1)} %get-tuple-element.5), channel_id=1, source_target_pairs={{0,1},{1,2},{2,3},{4,5},{5,6},{6,7},{8,9},{9,10},{10,11},{12,13},{... | collective-permute-start | bytes 2359304 | tf_op jit(solution)/shard_map/ppermute | solution.py:34
  34.9 20.6 %collective-permute-start.2 = (bf16[3072,128]{1,0:T(8,128)(2,1)S(1)}, bf16[3072,128]{1,0:T(8,128)(2,1)S(1)}, u32[]{:S(2)}, u32[]{:S(2)}) collective-permute-start(bf16[3072,128]{1,0:T(8,128)(2,1)S(1)} %collective-permute-done.1), channel_id=1, source_target_pairs={{1,0},{2,1},{3,2},{5,4},{6,5},{7,6},{9,8},{10,9},{11,10},{13,12},{... | collective-permute-start | bytes 2359304 | tf_op jit(solution)/shard_map/ppermute | solution.py:35
  36.2 20.6 %collective-permute-start.4 = (bf16[3072,128]{1,0:T(8,128)(2,1)S(1)}, bf16[3072,128]{1,0:T(8,128)(2,1)S(1)}, u32[]{:S(2)}, u32[]{:S(2)}) collective-permute-start(bf16[3072,128]{1,0:T(8,128)(2,1)S(1)} %collective-permute-done), channel_id=1, source_target_pairs={{0,1},{1,2},{2,3},{4,5},{5,6},{6,7},{8,9},{9,10},{10,11},{12,13},{... | collective-permute-start | bytes 2359304 | tf_op jit(solution)/shard_map/ppermute | solution.py:34
  55.5 19.7 %collective-permute-start.3 = (bf16[3072,128]{1,0:T(8,128)(2,1)S(1)}, bf16[3072,128]{1,0:T(8,128)(2,1)S(1)}, u32[]{:S(2)}, u32[]{:S(2)}) collective-permute-start(bf16[3072,128]{1,0:T(8,128)(2,1)S(1)} %collective-permute-done.2), channel_id=1, source_target_pairs={{1,0},{2,1},{3,2},{5,4},{6,5},{7,6},{9,8},{10,9},{11,10},{13,12},{... | collective-permute-start | bytes 2359304 | tf_op jit(solution)/shard_map/ppermute | solution.py:35
  56.8 19.6 %collective-permute-start.5 = (bf16[3072,128]{1,0:T(8,128)(2,1)S(1)}, bf16[3072,128]{1,0:T(8,128)(2,1)S(1)}, u32[]{:S(2)}, u32[]{:S(2)}) collective-permute-start(bf16[3072,128]{1,0:T(8,128)(2,1)S(1)} %collective-permute-done.4), channel_id=1, source_target_pairs={{0,1},{1,2},{2,3},{4,5},{5,6},{6,7},{8,9},{9,10},{10,11},{12,13},{... | collective-permute-start | bytes 2359304 | tf_op jit(solution)/shard_map/ppermute | solution.py:34
  102.9 170.9 %reduce-scatter.6.cloned.1.call-start = ((), (), s32[]{:S(2)}) async-start(), calls=%async_computation.4 | async-start | bytes 7077888 | tf_op jit(solution)/shard_map/reduce_scatter | solution.py:44
  102.9 19.6 %collective-permute-start.14 = (bf16[3072,128]{1,0:T(8,128)(2,1)}, bf16[3072,128]{1,0:T(8,128)(2,1)S(1)}, u32[]{:S(2)}, u32[]{:S(2)}) collective-permute-start(bf16[3072,128]{1,0:T(8,128)(2,1)} %get-tuple-element.7), channel_id=1, source_target_pairs={{1,0},{2,1},{3,2},{5,4},{6,5},{7,6},{9,8},{10,9},{11,10},{13,12},{... | collective-permute-start | bytes 2359304 | tf_op jit(solution)/shard_map/ppermute | solution.py:35
  104.2 19.6 %collective-permute-start.13 = (bf16[3072,128]{1,0:T(8,128)(2,1)}, bf16[3072,128]{1,0:T(8,128)(2,1)S(1)}, u32[]{:S(2)}, u32[]{:S(2)}) collective-permute-start(bf16[3072,128]{1,0:T(8,128)(2,1)} %get-tuple-element.7), channel_id=1, source_target_pairs={{0,1},{1,2},{2,3},{4,5},{5,6},{6,7},{8,9},{9,10},{10,11},{12,13},{... | collective-permute-start | bytes 2359304 | tf_op jit(solution)/shard_map/ppermute | solution.py:34
  122.5 18.0 %collective-permute-start.15 = (bf16[3072,128]{1,0:T(8,128)(2,1)S(1)}, bf16[3072,128]{1,0:T(8,128)(2,1)S(1)}, u32[]{:S(2)}, u32[]{:S(2)}) collective-permute-start(bf16[3072,128]{1,0:T(8,128)(2,1)S(1)} %collective-permute-done.14), channel_id=1, source_target_pairs={{1,0},{2,1},{3,2},{5,4},{6,5},{7,6},{9,8},{10,9},{11,10},{13,12},{... | collective-permute-start | bytes 2359304 | tf_op jit(solution)/shard_map/ppermute | solution.py:35
  123.8 18.0 %collective-permute-start.17 = (bf16[3072,128]{1,0:T(8,128)(2,1)S(1)}, bf16[3072,128]{1,0:T(8,128)(2,1)S(1)}, u32[]{:S(2)}, u32[]{:S(2)}) collective-permute-start(bf16[3072,128]{1,0:T(8,128)(2,1)S(1)} %collective-permute-done.13), channel_id=1, source_target_pairs={{0,1},{1,2},{2,3},{4,5},{5,6},{6,7},{8,9},{9,10},{10,11},{12,13},{... | collective-permute-start | bytes 2359304 | tf_op jit(solution)/shard_map/ppermute | solution.py:34
  140.5 17.3 %collective-permute-start.16 = (bf16[3072,128]{1,0:T(8,128)(2,1)S(1)}, bf16[3072,128]{1,0:T(8,128)(2,1)S(1)}, u32[]{:S(2)}, u32[]{:S(2)}) collective-permute-start(bf16[3072,128]{1,0:T(8,128)(2,1)S(1)} %collective-permute-done.15), channel_id=1, source_target_pairs={{1,0},{2,1},{3,2},{5,4},{6,5},{7,6},{9,8},{10,9},{11,10},{13,12},{... | collective-permute-start | bytes 2359304 | tf_op jit(solution)/shard_map/ppermute | solution.py:35
  141.8 17.2 %collective-permute-start.18 = (bf16[3072,128]{1,0:T(8,128)(2,1)S(1)}, bf16[3072,128]{1,0:T(8,128)(2,1)S(1)}, u32[]{:S(2)}, u32[]{:S(2)}) collective-permute-start(bf16[3072,128]{1,0:T(8,128)(2,1)S(1)} %collective-permute-done.17), channel_id=1, source_target_pairs={{0,1},{1,2},{2,3},{4,5},{5,6},{6,7},{8,9},{9,10},{10,11},{12,13},{... | collective-permute-start | bytes 2359304 | tf_op jit(solution)/shard_map/ppermute | solution.py:34
  147.1 12.1 %copy-start.1 = (bf16[3072,128]{1,0:T(8,128)(2,1)}, bf16[3072,128]{1,0:T(8,128)(2,1)S(1)}, u32[]{:S(2)}) copy-start(bf16[3072,128]{1,0:T(8,128)(2,1)S(1)} %add.225) | copy-start | bytes 2359300
  158.0 1.2 copy-start.3
  158.0 2.1 copy-start.15
  159.2 0.9 copy-start.5
  186.5 141.8 %reduce-scatter.8.cloned.1.call-start = ((), (), s32[]{:S(2)}) async-start(), calls=%async_computation.5 | async-start | bytes 7077888 | tf_op jit(solution)/shard_map/reduce_scatter | solution.py:44
  186.5 18.2 %collective-permute-start.27 = (bf16[3072,128]{1,0:T(8,128)(2,1)S(1)}, bf16[3072,128]{1,0:T(8,128)(2,1)S(1)}, u32[]{:S(2)}, u32[]{:S(2)}) collective-permute-start(bf16[3072,128]{1,0:T(8,128)(2,1)S(1)} %get-tuple-element.6), channel_id=1, source_target_pairs={{1,0},{2,1},{3,2},{5,4},{6,5},{7,6},{9,8},{10,9},{11,10},{13,12},{... | collective-permute-start | bytes 2359304 | tf_op jit(solution)/shard_map/ppermute | solution.py:35
  187.8 18.2 %collective-permute-start.26 = (bf16[3072,128]{1,0:T(8,128)(2,1)S(1)}, bf16[3072,128]{1,0:T(8,128)(2,1)S(1)}, u32[]{:S(2)}, u32[]{:S(2)}) collective-permute-start(bf16[3072,128]{1,0:T(8,128)(2,1)S(1)} %get-tuple-element.6), channel_id=1, source_target_pairs={{0,1},{1,2},{2,3},{4,5},{5,6},{6,7},{8,9},{9,10},{10,11},{12,13},{... | collective-permute-start | bytes 2359304 | tf_op jit(solution)/shard_map/ppermute | solution.py:34
  204.8 17.7 %collective-permute-start.28 = (bf16[3072,128]{1,0:T(8,128)(2,1)S(1)}, bf16[3072,128]{1,0:T(8,128)(2,1)S(1)}, u32[]{:S(2)}, u32[]{:S(2)}) collective-permute-start(bf16[3072,128]{1,0:T(8,128)(2,1)S(1)} %collective-permute-done.27), channel_id=1, source_target_pairs={{1,0},{2,1},{3,2},{5,4},{6,5},{7,6},{9,8},{10,9},{11,10},{13,12},{... | collective-permute-start | bytes 2359304 | tf_op jit(solution)/shard_map/ppermute | solution.py:35
  206.1 17.7 %collective-permute-start.30 = (bf16[3072,128]{1,0:T(8,128)(2,1)S(1)}, bf16[3072,128]{1,0:T(8,128)(2,1)S(1)}, u32[]{:S(2)}, u32[]{:S(2)}) collective-permute-start(bf16[3072,128]{1,0:T(8,128)(2,1)S(1)} %collective-permute-done.26), channel_id=1, source_target_pairs={{0,1},{1,2},{2,3},{4,5},{5,6},{6,7},{8,9},{9,10},{10,11},{12,13},{... | collective-permute-start | bytes 2359304 | tf_op jit(solution)/shard_map/ppermute | solution.py:34
  222.5 14.6 %collective-permute-start.29 = (bf16[3072,128]{1,0:T(8,128)(2,1)S(1)}, bf16[3072,128]{1,0:T(8,128)(2,1)S(1)}, u32[]{:S(2)}, u32[]{:S(2)}) collective-permute-start(bf16[3072,128]{1,0:T(8,128)(2,1)S(1)} %collective-permute-done.28), channel_id=1, source_target_pairs={{1,0},{2,1},{3,2},{5,4},{6,5},{7,6},{9,8},{10,9},{11,10},{13,12},{... | collective-permute-start | bytes 2359304 | tf_op jit(solution)/shard_map/ppermute | solution.py:35
  223.8 14.5 %collective-permute-start.31 = (bf16[3072,128]{1,0:T(8,128)(2,1)S(1)}, bf16[3072,128]{1,0:T(8,128)(2,1)S(1)}, u32[]{:S(2)}, u32[]{:S(2)}) collective-permute-start(bf16[3072,128]{1,0:T(8,128)(2,1)S(1)} %collective-permute-done.30), channel_id=1, source_target_pairs={{0,1},{1,2},{2,3},{4,5},{5,6},{6,7},{8,9},{9,10},{10,11},{12,13},{... | collective-permute-start | bytes 2359304 | tf_op jit(solution)/shard_map/ppermute | solution.py:34
  228.8 9.7 %copy-start.7 = (bf16[3072,128]{1,0:T(8,128)(2,1)}, bf16[3072,128]{1,0:T(8,128)(2,1)S(1)}, u32[]{:S(2)}) copy-start(bf16[3072,128]{1,0:T(8,128)(2,1)S(1)} %add.228) | copy-start | bytes 2359300
  237.3 1.2 copy-start.9
  268.1 62.2 %collective-permute-start.6 = (bf16[768,128]{0,1:T(8,128)(2,1)}, bf16[768,128]{0,1:T(8,128)(2,1)S(1)}, u32[]{:S(2)}, u32[]{:S(2)}) collective-permute-start(bf16[768,128]{0,1:T(8,128)(2,1)} %get-tuple-element.19), channel_id=1, source_target_pairs={{0,3},{1,0},{2,1},{3,2},{4,7},{5,4},{6,5},{7,6},{8,11},{9,8},{10,9... | collective-permute-start | bytes 589832 | tf_op jit(solution)/shard_map/ppermute | solution.py:48
  272.2 59.6 %collective-permute-start.7 = (bf16[768,128]{0,1:T(8,128)(2,1)}, bf16[768,128]{0,1:T(8,128)(2,1)S(1)}, u32[]{:S(2)}, u32[]{:S(2)}) collective-permute-start(bf16[768,128]{0,1:T(8,128)(2,1)} %get-tuple-element.18), channel_id=1, source_target_pairs={{0,2},{1,3},{2,0},{3,1},{4,6},{5,7},{6,4},{7,5},{8,10},{9,11},{10,... | collective-permute-start | bytes 589832 | tf_op jit(solution)/shard_map/ppermute | solution.py:48
  272.2 61.9 %collective-permute-start.8 = (bf16[768,128]{0,1:T(8,128)(2,1)}, bf16[768,128]{0,1:T(8,128)(2,1)}, u32[]{:S(2)}, u32[]{:S(2)}) collective-permute-start(bf16[768,128]{0,1:T(8,128)(2,1)} %get-tuple-element.17), channel_id=1, source_target_pairs={{0,1},{1,2},{2,3},{3,0},{4,5},{5,6},{6,7},{7,4},{8,9},{9,10},{10,1... | collective-permute-start | bytes 589832 | tf_op jit(solution)/shard_map/ppermute | solution.py:48
  276.0 59.8 %collective-permute-start.19 = (bf16[768,128]{0,1:T(8,128)(2,1)}, bf16[768,128]{0,1:T(8,128)(2,1)S(1)}, u32[]{:S(2)}, u32[]{:S(2)}) collective-permute-start(bf16[768,128]{0,1:T(8,128)(2,1)} %get-tuple-element.31), channel_id=1, source_target_pairs={{0,3},{1,0},{2,1},{3,2},{4,7},{5,4},{6,5},{7,6},{8,11},{9,8},{10,9... | collective-permute-start | bytes 589832 | tf_op jit(solution)/shard_map/ppermute | solution.py:48
  278.1 63.2 %collective-permute-start.20 = (bf16[768,128]{0,1:T(8,128)(2,1)}, bf16[768,128]{0,1:T(8,128)(2,1)}, u32[]{:S(2)}, u32[]{:S(2)}) collective-permute-start(bf16[768,128]{0,1:T(8,128)(2,1)} %get-tuple-element.30), channel_id=1, source_target_pairs={{0,2},{1,3},{2,0},{3,1},{4,6},{5,7},{6,4},{7,5},{8,10},{9,11},{10,... | collective-permute-start | bytes 589832 | tf_op jit(solution)/shard_map/ppermute | solution.py:48
  330.3 12.4 %collective-permute-start.21 = (bf16[768,128]{0,1:T(8,128)(2,1)}, bf16[768,128]{0,1:T(8,128)(2,1)}, u32[]{:S(2)}, u32[]{:S(2)}) collective-permute-start(bf16[768,128]{0,1:T(8,128)(2,1)} %get-tuple-element.29), channel_id=1, source_target_pairs={{0,1},{1,2},{2,3},{3,0},{4,5},{5,6},{6,7},{7,4},{8,9},{9,10},{10,1... | collective-permute-start | bytes 589832 | tf_op jit(solution)/shard_map/ppermute | solution.py:48
  331.8 14.1 %collective-permute-start.32 = (bf16[768,128]{0,1:T(8,128)(2,1)}, bf16[768,128]{0,1:T(8,128)(2,1)}, u32[]{:S(2)}, u32[]{:S(2)}) collective-permute-start(bf16[768,128]{0,1:T(8,128)(2,1)} %get-tuple-element.43), channel_id=1, source_target_pairs={{0,3},{1,0},{2,1},{3,2},{4,7},{5,4},{6,5},{7,6},{8,11},{9,8},{10,9... | collective-permute-start | bytes 589832 | tf_op jit(solution)/shard_map/ppermute | solution.py:48
  334.2 21.6 %collective-permute-start.33 = (bf16[768,128]{0,1:T(8,128)(2,1)}, bf16[768,128]{0,1:T(8,128)(2,1)}, u32[]{:S(2)}, u32[]{:S(2)}) collective-permute-start(bf16[768,128]{0,1:T(8,128)(2,1)} %get-tuple-element.42), channel_id=1, source_target_pairs={{0,2},{1,3},{2,0},{3,1},{4,6},{5,7},{6,4},{7,5},{8,10},{9,11},{10,... | collective-permute-start | bytes 589832 | tf_op jit(solution)/shard_map/ppermute | solution.py:48
  336.5 22.7 %collective-permute-start.34 = (bf16[768,128]{0,1:T(8,128)(2,1)}, bf16[768,128]{0,1:T(8,128)(2,1)}, u32[]{:S(2)}, u32[]{:S(2)}) collective-permute-start(bf16[768,128]{0,1:T(8,128)(2,1)} %get-tuple-element.41), channel_id=1, source_target_pairs={{0,1},{1,2},{2,3},{3,0},{4,5},{5,6},{6,7},{7,4},{8,9},{9,10},{10,1... | collective-permute-start | bytes 589832 | tf_op jit(solution)/shard_map/ppermute | solution.py:48
  341.3 28.1 %collective-permute-start.11 = (bf16[768,128]{1,0:T(8,128)(2,1)}, bf16[768,128]{1,0:T(8,128)(2,1)}, u32[]{:S(2)}, u32[]{:S(2)}) collective-permute-start(bf16[768,128]{1,0:T(8,128)(2,1)} %bitcast.197), channel_id=1, source_target_pairs={{0,16},{4,24},{8,0},{12,8},{16,20},{20,28},{24,4},{28,12},{1,17},{... | collective-permute-start | bytes 589832 | tf_op jit(solution)/shard_map/ppermute | solution.py:55
  342.8 30.0 %collective-permute-start.12 = (bf16[768,128]{1,0:T(8,128)(2,1)}, bf16[768,128]{1,0:T(8,128)(2,1)}, u32[]{:S(2)}, u32[]{:S(2)}) collective-permute-start(bf16[768,128]{1,0:T(8,128)(2,1)} %bitcast.12), channel_id=1, source_target_pairs={{0,24},{4,0},{8,8},{12,16},{16,28},{20,4},{24,12},{28,20},{1,25},{... | collective-permute-start | bytes 589832 | tf_op jit(solution)/shard_map/ppermute | solution.py:55
  345.9 26.9 %collective-permute-start.9 = (bf16[768,128]{1,0:T(8,128)(2,1)}, bf16[768,128]{1,0:T(8,128)(2,1)}, u32[]{:S(2)}, u32[]{:S(2)}) collective-permute-start(bf16[768,128]{1,0:T(8,128)(2,1)} %bitcast.6), channel_id=1, source_target_pairs={{0,0},{4,8},{8,16},{12,24},{16,4},{20,12},{24,20},{28,28},{1,1},{5... | collective-permute-start | bytes 589832 | tf_op jit(solution)/shard_map/ppermute | solution.py:55
  355.8 20.8 %collective-permute-start.10 = (bf16[768,128]{1,0:T(8,128)(2,1)}, bf16[768,128]{1,0:T(8,128)(2,1)}, u32[]{:S(2)}, u32[]{:S(2)}) collective-permute-start(bf16[768,128]{1,0:T(8,128)(2,1)} %bitcast.8), channel_id=1, source_target_pairs={{0,8},{4,16},{8,24},{12,0},{16,12},{20,20},{24,28},{28,4},{1,9},{5... | collective-permute-start | bytes 589832 | tf_op jit(solution)/shard_map/ppermute | solution.py:55
  363.0 17.7 %collective-permute-start.22 = (bf16[768,128]{1,0:T(8,128)(2,1)}, bf16[768,128]{1,0:T(8,128)(2,1)}, u32[]{:S(2)}, u32[]{:S(2)}) collective-permute-start(bf16[768,128]{1,0:T(8,128)(2,1)} %bitcast.201), channel_id=1, source_target_pairs={{0,0},{4,8},{8,16},{12,24},{16,4},{20,12},{24,20},{28,28},{1,1},{5... | collective-permute-start | bytes 589832 | tf_op jit(solution)/shard_map/ppermute | solution.py:55
  369.4 16.0 %collective-permute-start.23 = (bf16[768,128]{1,0:T(8,128)(2,1)}, bf16[768,128]{1,0:T(8,128)(2,1)S(1)}, u32[]{:S(2)}, u32[]{:S(2)}) collective-permute-start(bf16[768,128]{1,0:T(8,128)(2,1)} %bitcast.200), channel_id=1, source_target_pairs={{0,8},{4,16},{8,24},{12,0},{16,12},{20,20},{24,28},{28,4},{1,9},{5... | collective-permute-start | bytes 589832 | tf_op jit(solution)/shard_map/ppermute | solution.py:55
  372.8 12.8 %collective-permute-start.24 = (bf16[768,128]{1,0:T(8,128)(2,1)}, bf16[768,128]{1,0:T(8,128)(2,1)S(1)}, u32[]{:S(2)}, u32[]{:S(2)}) collective-permute-start(bf16[768,128]{1,0:T(8,128)(2,1)} %bitcast.199), channel_id=1, source_target_pairs={{0,16},{4,24},{8,0},{12,8},{16,20},{20,28},{24,4},{28,12},{1,17},{... | collective-permute-start | bytes 589832 | tf_op jit(solution)/shard_map/ppermute | solution.py:55
  372.9 15.9 %collective-permute-start.25 = (bf16[768,128]{1,0:T(8,128)(2,1)S(1)}, bf16[768,128]{1,0:T(8,128)(2,1)S(1)}, u32[]{:S(2)}, u32[]{:S(2)}) collective-permute-start(bf16[768,128]{1,0:T(8,128)(2,1)S(1)} %bitcast.198), channel_id=1, source_target_pairs={{0,24},{4,0},{8,8},{12,16},{16,28},{20,4},{24,12},{28,20},{1,25},{... | collective-permute-start | bytes 589832 | tf_op jit(solution)/shard_map/ppermute | solution.py:55
  376.6 17.2 %collective-permute-start.35 = (bf16[768,128]{1,0:T(8,128)(2,1)S(1)}, bf16[768,128]{1,0:T(8,128)(2,1)S(1)}, u32[]{:S(2)}, u32[]{:S(2)}) collective-permute-start(bf16[768,128]{1,0:T(8,128)(2,1)S(1)} %bitcast.196), channel_id=1, source_target_pairs={{0,0},{4,8},{8,16},{12,24},{16,4},{20,12},{24,20},{28,28},{1,1},{5... | collective-permute-start | bytes 589832 | tf_op jit(solution)/shard_map/ppermute | solution.py:55
  377.5 1.5 copy-start.18
  380.7 13.2 %collective-permute-start.36 = (bf16[768,128]{1,0:T(8,128)(2,1)S(1)}, bf16[768,128]{1,0:T(8,128)(2,1)S(1)}, u32[]{:S(2)}, u32[]{:S(2)}) collective-permute-start(bf16[768,128]{1,0:T(8,128)(2,1)S(1)} %bitcast.195), channel_id=1, source_target_pairs={{0,8},{4,16},{8,24},{12,0},{16,12},{20,20},{24,28},{28,4},{1,9},{5... | collective-permute-start | bytes 589832 | tf_op jit(solution)/shard_map/ppermute | solution.py:55
  385.5 8.4 %collective-permute-start.37 = (bf16[768,128]{1,0:T(8,128)(2,1)S(1)}, bf16[768,128]{1,0:T(8,128)(2,1)S(1)}, u32[]{:S(2)}, u32[]{:S(2)}) collective-permute-start(bf16[768,128]{1,0:T(8,128)(2,1)S(1)} %bitcast.194), channel_id=1, source_target_pairs={{0,16},{4,24},{8,0},{12,8},{16,20},{20,28},{24,4},{28,12},{1,17},{... | collective-permute-start | bytes 589832 | tf_op jit(solution)/shard_map/ppermute | solution.py:55
  385.6 8.2 %collective-permute-start.38 = (bf16[768,128]{1,0:T(8,128)(2,1)S(1)}, bf16[768,128]{1,0:T(8,128)(2,1)S(1)}, u32[]{:S(2)}, u32[]{:S(2)}) collective-permute-start(bf16[768,128]{1,0:T(8,128)(2,1)S(1)} %bitcast.193), channel_id=1, source_target_pairs={{0,24},{4,0},{8,8},{12,16},{16,28},{20,4},{24,12},{28,20},{1,25},{... | collective-permute-start | bytes 589832 | tf_op jit(solution)/shard_map/ppermute | solution.py:55
  388.8 1.2 copy-start.16
  390.0 1.1 copy-start.4
  391.1 1.1 copy-start.2
  392.3 1.1 copy-start.6
  393.8 1.1 copy-start.14
  395.0 1.1 copy-start.10
  396.1 1.1 copy-start.8
  397.2 1.1 copy-start.12
  399.8 1.8 collective-permute-start.39
  401.8 11.2 %collective-permute-start.40 = (bf16[3,512,128]{2,1,0:T(8,128)(2,1)S(1)}, bf16[3,512,128]{2,1,0:T(8,128)(2,1)S(1)}, u32[]{:S(2)}, u32[]{:S(2)}) collective-permute-start(bf16[3,512,128]{2,1,0:T(8,128)(2,1)S(1)} %add_convert_fusion.1), channel_id=1, source_target_pairs={{0,8},{4,12},{8,0},{12,4},{16,24},{20,28},{24,16},{28,20},{1,9},{5... | collective-permute-start | bytes 1179656 | tf_op jit(solution)/shard_map/ppermute | solution.py:75
  413.1 10.4 %copy-start = (f32[3,512,128]{2,1,0:T(8,128)S(1)}, f32[3,512,128]{2,1,0:T(8,128)}, u32[]{:S(2)}) copy-start(f32[3,512,128]{2,1,0:T(8,128)} %param.7) | copy-start | bytes 2359300
  413.1 10.4 %collective-permute-start.41 = (bf16[3,512,128]{2,1,0:T(8,128)(2,1)S(1)}, bf16[3,512,128]{2,1,0:T(8,128)(2,1)S(1)}, u32[]{:S(2)}, u32[]{:S(2)}) collective-permute-start(bf16[3,512,128]{2,1,0:T(8,128)(2,1)S(1)} %add_convert_fusion), channel_id=1, source_target_pairs={{0,16},{4,20},{8,24},{12,28},{16,0},{20,4},{24,8},{28,12},{1,17},{... | collective-permute-start | bytes 1179656 | tf_op jit(solution)/shard_map/ppermute | solution.py:75
  (3 other events, 2.2 us)
Sparse Core Ops, SparseCore 0:
  103.0 63.4 reduce-scatter.3
  186.6 62.3 reduce-scatter.5
  265.8 62.3 reduce-scatter.7

commit v2 on v1

--- a/solution.py
+++ b/solution.py
@@ -1,6 +1,8 @@
 import jax
 import jax.numpy as jnp
 from jax import lax
+from jax.experimental import pallas as pl
+from jax.experimental.pallas import tpu as pltpu
 from jax.sharding import PartitionSpec as P
 
 
@@ -9,7 +11,7 @@
     return jnp.repeat(listed.astype(jnp.float32), tile_rows, axis=1)
 
 
-def on_device(resident_inverse, factor, diag_inverse, anc_tiles, slot_tile):
+def plain(resident_inverse, factor, diag_inverse, anc_tiles, slot_tile):
     own_rows, own_cols = resident_inverse.shape
     supers, _, part_width = factor.shape
     row_index = lax.axis_index("row")
@@ -77,6 +79,348 @@
         step *= 2
     return (jnp.stack(news), diag_inverse + totals)
 
+MESH = pl.DeviceIdType.MESH
+BF = jnp.bfloat16
+F32 = jnp.float32
+CORES = 2
+SIDE = 2
+CHIPS = SIDE * SIDE
+
+
+def sweep(row_count, col_count, supers, mine_ref, matrix_ref, y_ref, t_ref,
+          slab, parts, to_core, from_core, to_chip, from_chip, block_y, passed, own_y, to_sum, from_sum,
+          slab_sem, own_sem, ag_send, ag_recv, core_send, core_recv, chip_send, chip_recv,
+          col_send, col_recv, row_send, row_recv, sum_send, sum_recv):
+    row = lax.axis_index("row")
+    col = lax.axis_index("col")
+    last = col_count - 1
+    core = row % CORES
+    chip = row // CORES
+    x, y = chip % SIDE, chip // SIDE
+    half = col // 2
+    width = parts.shape[2] // 2
+    piece = slab.shape[2]
+    owners = row_count // CORES
+    passes = 2 * supers
+
+    barrier = pltpu.get_barrier_semaphore()
+
+    @pl.loop(1, row_count)
+    def _(by):
+        pl.semaphore_signal(barrier, inc=1, device_id=((row + by) % row_count, col), device_id_type=MESH)
+
+    @pl.loop(1, col_count)
+    def _(by):
+        pl.semaphore_signal(barrier, inc=1, device_id=(row, (col + by) % col_count), device_id_type=MESH)
+
+    pl.semaphore_wait(barrier, row_count - 1 + last)
+
+    def to(src, dst, send, recv, r, c):
+        return pltpu.make_async_remote_copy(
+            src_ref=src, dst_ref=dst, send_sem=send, recv_sem=recv, device_id=(r, c), device_id_type=MESH
+        )
+
+    def landed(ref, sem):
+        pltpu.make_async_copy(ref, ref, sem).wait()
+
+    def part(s, w):
+        return parts.at[s, w // 2, pl.ds(pl.multiple_of((w % 2) * width, width), width), :]
+
+    def gather(s, w, way, src):
+        return to(src, part(s, w), ag_send.at[way, s, w], ag_recv.at[s, w], row, col + (1 - 2 * way))
+
+    def chip_at(k):
+        xk = (x + 1 - k // 2) % 2
+        yk = (y + 1 - k % 2) % 2
+        return yk * SIDE + xk
+
+    def slab_copy(k, own, slot):
+        which = chip_at(k) * CORES + (core + 1 - own) % CORES
+        off = pl.multiple_of(which * piece, piece)
+        return pltpu.make_async_copy(matrix_ref.at[:, pl.ds(off, piece)], slab.at[slot], slab_sem.at[slot])
+
+    def own_part(s):
+        return pltpu.make_async_copy(mine_ref.at[s], part(s, col), own_sem.at[s])
+
+    slab_copy(0, 0, 0).start()
+
+    @pl.loop(0, supers)
+    def _(s):
+        @pl.when(col < last)
+        def _():
+            gather(s, col, 0, mine_ref.at[s]).start()
+
+        @pl.when(col > 0)
+        def _():
+            gather(s, col, 1, mine_ref.at[s]).start()
+
+        own_part(s).start()
+
+    def arrive(d, s):
+        @pl.when(col >= d)
+        def _():
+            landed(part(s, col - d), ag_recv.at[s, col - d])
+
+            @pl.when(col < last)
+            def _():
+                gather(s, col - d, 0, part(s, col - d)).start()
+
+        @pl.when(col + d <= last)
+        def _():
+            landed(part(s, col + d), ag_recv.at[s, col + d])
+
+            @pl.when(col > 0)
+            def _():
+                gather(s, col + d, 1, part(s, col + d)).start()
+
+    def core_copy(p, k):
+        return to(to_core.at[p % 2, k], from_core.at[p, k], core_send.at[p % 2, k], core_recv.at[p, k],
+                  chip * CORES + 1 - core, col)
+
+    def chip_copy(p, k):
+        return to(to_chip.at[p % 2, k], from_chip.at[p, k], chip_send.at[p % 2, k], chip_recv.at[p, k],
+                  chip_at(k) * CORES + core, col)
+
+    def finish(p):
+        total = to_chip[p % 2, CHIPS - 1].astype(F32)
+        for k in range(CHIPS - 1):
+            landed(from_chip.at[p, k], chip_recv.at[p, k])
+            total = total + from_chip[p, k].astype(F32)
+        block_y[p] = total.astype(BF)
+
+    def col_copies(p, act):
+        s, h = p % supers, p // supers
+        pair = (half + h) % 2
+        for j in range(2):
+            w = pair * 2 + j
+            src = block_y.at[p, pl.ds(j * width, width), :]
+            remote = to(src, passed.at[s, col], col_send.at[p, j], col_recv.at[s, col], row, w)
+            if act == "start":
+                @pl.when(w != col)
+                def _():
+                    remote.start()
+
+                @pl.when(w == col)
+                def _():
+                    pltpu.make_async_copy(src, passed.at[s, col], col_recv.at[s, col]).start()
+            else:
+                @pl.when(w != col)
+                def _():
+                    remote.wait_send()
+
+    def row_copies(p, act):
+        s, h = p % supers, p // supers
+        pair = (half + h) % 2
+        for j in range(2):
+            c = pair * 2 + j
+            dest = CORES * c + row // owners
+            q = row % owners
+            remote = to(passed.at[s, c], own_y.at[s, q], row_send.at[s, c], row_recv.at[s, q], dest, col)
+            if act == "start":
+                landed(passed.at[s, c], col_recv.at[s, c])
+
+                @pl.when(dest != row)
+                def _():
+                    remote.start()
+
+                @pl.when(dest == row)
+                def _():
+                    pltpu.make_async_copy(passed.at[s, c], own_y.at[s, q], row_recv.at[s, q]).start()
+            else:
+                @pl.when(dest != row)
+                def _():
+                    remote.wait_send()
+
+    @pl.loop(0, passes)
+    def _(p):
+        s, h = p % supers, p // supers
+        pair = (half + h) % 2
+
+        @pl.when(h == 0)
+        def _():
+            landed(part(s, col), own_sem.at[s])
+            arrive(1, s)
+
+        @pl.when(h == 1)
+        def _():
+            arrive(2, s)
+            arrive(3, s)
+
+        @pl.when((p == 2) | (p == 3))
+        def _():
+            finish(p - 2)
+
+        @pl.when(p >= 3)
+        def _():
+            finish(p - 1)
+
+        @pl.when(p == passes - 1)
+        def _():
+            @pl.loop(0, passes - 1)
+            def _(e):
+                col_copies(e, "start")
+
+        @pl.loop(0, CHIPS)
+        def _(k):
+            @pl.when(p >= 2)
+            def _():
+                core_copy(p - 2, k).wait_send()
+
+                @pl.when(k < CHIPS - 1)
+                def _():
+                    chip_copy(p - 2, k).wait_send()
+
+            landed(slab.at[0], slab_sem.at[0])
+            slab_copy(k, 1, 1).start()
+            to_core[p % 2, k] = jnp.dot(parts[s, pair], slab[0], preferred_element_type=F32).astype(BF)
+
+            @pl.when(k > 0)
+            def _():
+                chip_copy(p, k - 1).start()
+
+            landed(slab.at[1], slab_sem.at[1])
+
+            @pl.when((k < CHIPS - 1) | (p < passes - 1))
+            def _():
+                slab_copy((k + 1) % CHIPS, 0, 0).start()
+
+            core_copy(p, k).start()
+            mine = jnp.dot(parts[s, pair], slab[1], preferred_element_type=F32)
+            landed(from_core.at[p, k], core_recv.at[p, k])
+            to_chip[p % 2, k] = (mine + from_core[p, k].astype(F32)).astype(BF)
+
+    finish(passes - 1)
+
+    @pl.loop(0, passes - 1)
+    def _(e):
+        row_copies(e, "start")
+
+    col_copies(passes - 1, "start")
+    row_copies(passes - 1, "start")
+
+    partners = [
+        chip * CORES + 1 - core,
+        (y * SIDE + 1 - x) * CORES + core,
+        ((1 - y) * SIDE + x) * CORES + core,
+    ]
+    stages = len(partners)
+
+    def sum_copy(s, stage):
+        return to(to_sum.at[s, stage], from_sum.at[s, stage], sum_send.at[s, stage], sum_recv.at[s, stage],
+                  partners[stage], col)
+
+    @pl.loop(0, supers)
+    def _(s):
+        t_ref[s] = jnp.zeros(t_ref.shape[1:], F32)
+        for q in range(owners):
+            landed(own_y.at[s, q], row_recv.at[s, q])
+            here = own_y[s, q]
+            y_ref[s, pl.ds(q * piece, piece), :] = here.astype(F32).T.astype(BF)
+            for pr in range(2):
+                rows = pl.ds(pr * 2 * width, 2 * width)
+                t_ref[s, rows, :] += lax.dot_general(
+                    parts[s, pr, :, pl.ds(q * piece, piece)], here, (((1,), (1,)), ((), ())),
+                    preferred_element_type=F32,
+                )
+        to_sum[s, 0] = t_ref[s].astype(BF)
+
+    for stage in range(stages):
+        @pl.loop(0, supers)
+        def _(s):
+            sum_copy(s, stage).start()
+
+        @pl.loop(0, supers)
+        def _(s):
+            landed(from_sum.at[s, stage], sum_recv.at[s, stage])
+            total = to_sum[s, stage].astype(F32) + from_sum[s, stage].astype(F32)
+            if stage < stages - 1:
+                to_sum[s, stage + 1] = total.astype(BF)
+            else:
+                t_ref[s] = total
+
+    @pl.loop(0, supers)
+    def _(s):
+        for stage in range(stages):
+            sum_copy(s, stage).wait_send()
+
+        @pl.loop(0, col_count)
+        def _(w):
+            @pl.when((w <= col) & (col < last))
+            def _():
+                gather(s, w, 0, part(s, w)).wait_send()
+
+            @pl.when((w >= col) & (col > 0))
+            def _():
+                gather(s, w, 1, part(s, w)).wait_send()
+
+    @pl.loop(0, passes)
+    def _(p):
+        col_copies(p, "wait")
+        row_copies(p, "wait")
+
+        @pl.when(p >= passes - 2)
+        def _():
+            @pl.loop(0, CHIPS)
+            def _(k):
+                core_copy(p, k).wait_send()
+
+                @pl.when(k < CHIPS - 1)
+                def _():
+                    chip_copy(p, k).wait_send()
+
+
+def fused(resident_inverse, factor, diag_inverse, anc_tiles, slot_tile):
+    own_rows, own_cols = resident_inverse.shape
+    supers, _, width = factor.shape
+    row_count, col_count = lax.axis_size("row"), lax.axis_size("col")
+    total_rows = own_rows * row_count
+    row_mask = slot_rows(anc_tiles, slot_tile, total_rows // slot_tile.shape[0])
+    own_mask = lax.dynamic_slice_in_dim(row_mask, lax.axis_index("row") * own_rows, own_rows, 1).astype(BF)
+    mine = jnp.swapaxes(factor, 1, 2) * own_mask[:, None, :]
+    piece = own_cols // row_count
+    owners = row_count // CORES
+    passes = 2 * supers
+    wide = width * col_count
+    dma = pltpu.SemaphoreType.DMA
+    y, t = pl.pallas_call(
+        lambda *refs: sweep(row_count, col_count, supers, *refs),
+        out_shape=(
+            jax.ShapeDtypeStruct((supers, own_rows, width), BF),
+            jax.ShapeDtypeStruct((supers, wide, width), F32),
+        ),
+        in_specs=[pl.BlockSpec(memory_space=pl.ANY)] * 2,
+        out_specs=[pl.BlockSpec(memory_space=pltpu.VMEM)] * 2,
+        scratch_shapes=[
+            pltpu.VMEM((2, own_rows, piece), BF),
+            pltpu.VMEM((supers, 2, 2 * width, own_rows), BF),
+            pltpu.VMEM((2, CHIPS, 2 * width, piece), BF),
+            pltpu.VMEM((passes, CHIPS, 2 * width, piece), BF),
+            pltpu.VMEM((2, CHIPS, 2 * width, piece), BF),
+            pltpu.VMEM((passes, CHIPS - 1, 2 * width, piece), BF),
+            pltpu.VMEM((passes, 2 * width, piece), BF),
+            pltpu.VMEM((supers, col_count, width, piece), BF),
+            pltpu.VMEM((supers, owners, width, piece), BF),
+            pltpu.VMEM((supers, 3, wide, width), BF),
+            pltpu.VMEM((supers, 3, wide, width), BF),
+            dma((2,)), dma((supers,)),
+            dma((2, supers, col_count)), dma((supers, col_count)),
+            dma((2, CHIPS)), dma((passes, CHIPS)),
+            dma((2, CHIPS)), dma((passes, CHIPS)),
+            dma((passes, 2)), dma((supers, col_count)),
+            dma((supers, col_count)), dma((supers, owners)),
+            dma((supers, 3)), dma((supers, 3)),
+        ],
+        compiler_params=pltpu.CompilerParams(
+            collective_id=0, has_side_effects=True, vmem_limit_bytes=67043328
+        ),
+    )(mine, resident_inverse)
+    return (-(y * own_mask[:, :, None]), diag_inverse + t)
+
+
+def on_device(*arrays):
+    square = lax.axis_size("row") == CHIPS * CORES and lax.axis_size("col") == CHIPS
+    return (fused if square else plain)(*arrays)
+
 
 def solution(mesh):
     placed = (P("row", "col"), P(None, "row", "col"), P(None, None, "col"), P(), P())

time: 440 us -> 288 us (0.65); the launches traced: 431 us -> 287 us
  Pallas kernels: 0 us -> 271 us
  waiting for transfers between devices: 190 us -> 0 us
  starting transfers between devices: 101 us -> 0 us
  matrix products: 83.7 us -> 0 us
  between operations: 15.1 us -> 0.72 us
  local copies, waits for them, and re-layouts: 24.4 us -> 10.3 us
  other arithmetic: 17.2 us -> 4.93 us
    pallas_call x0 -> x1, Pallas kernels: none -> 271 us  [fused(): pl.pallas_call(lambda *refs: sweep(row_count, col_count, supers, *refs),...]
    ppermute x42 -> x0, waiting for transfers between devices: 141 us -> none  [the longest x9 112 us: on_device(): downs.append(lax.ppermute(downs[-1], 'col', down_moves))]
    ppermute x42 -> x0, starting transfers between devices: 100 us -> none  [the longest x9 44 us: on_device(): ups.append(lax.ppermute(ups[-1], 'col', up_moves))]
    dot_general x15 -> x0, matrix products: 83.7 us -> none  [the longest x3 78.8 us: on_device(): lax.dot_general(resident_inverse, wide, (((0,), (0,)), ((), ())), preferr...]
    reduce_scatter x3 -> x0, waiting for transfers between devices: 49 us -> none  [on_device(): summed = lax.psum_scatter(partial, 'row', scatter_dimension=0, tiled=True)]
    dynamic_slice x17 -> x0, local copies, waits for them, and re-layouts: 9.5 us -> none  [the longest x14 9.31 us: on_device(): lax.dynamic_index_in_dim(got, (block - col_index) % col_count, 0, keepdim...]
    another operation x12 -> x0, other arithmetic: 7.87 us -> none  [the longest x3 3.46 us: on_device(): got = jnp.stack(got)]
    another operation x6 -> x0, local copies, waits for them, and re-layouts: 6.46 us -> none  [the longest x3 6.38 us: on_device(): got = jnp.stack(got)]
  transfers between devices with their start and end apart: 45 -> 0, of which waited for: 17 -> 0; matrix products, arithmetic and copies ran while one was open for 19% -> 0% of each run, Pallas kernels for 0% -> 0%
where the time goes in v2:
time: 288 us; the launch traced here: 287 us
  Pallas kernels  271 us (94%)
  local copies, waits for them, and re-layouts  10.3 us (4%)
  other arithmetic  4.93 us (2%)
    pallas_call x1, Pallas kernels, fused(): pl.pallas_call(lambda *refs: sweep(row_count, col_count, supers, *refs),...  271 us
    unnamed x12, local copies, waits for them, and re-layouts  7.48 us

profile of v2, /device:TPU:0, one launch (start us, length us, event | category | flops | bytes accessed | tf_op | source)
XLA Modules:
  0.0 286.6 jit_solution(18407147060458413484)
XLA Ops:
  0.6 0.8 compare_reduce_fusion
  1.5 0.1 broadcast_bitcast_fusion
  1.6 0.1 copy.13
  1.7 0.0 copy-start.2
  1.7 2.8 copy.10
  4.6 0.0 copy-done.2
  4.6 1.6 multiply_bitcast_fusion.refs_0_
  6.2 270.6 %shard_map.68 = (bf16[3,3072,128]{2,1,0:T(8,128)(2,1)}, f32[3,512,128]{2,1,0:T(8,128)}) custom-call(bf16[3,128,3072]{2,1,0:T(8,128)(2,1)} %multiply_bitcast_fusion.refs_0_, bf16[3072,6144]{1,0:T(8,128)(2,1)} %refs_1_.1), custom_call_target="tpu_custom_call" | custom-call | tf_op jit(solution)/shard_map/pallas_call | solution.py:385
  276.8 0.0 copy-start.3
  276.8 2.8 copy.11
  279.7 0.0 copy-done.3
  279.7 1.6 multiply_negate_fusion
  281.3 0.0 copy-start
  281.3 0.0 copy-start.1
  281.3 4.4 %copy.12 = bf16[3,3072,128]{2,1,0:T(8,128)(2,1)} copy(bf16[3,3072,128]{1,2,0:T(8,128)(2,1)} %multiply_negate_fusion) | data formatting | bytes 4718592
  285.6 0.0 copy-done
  285.7 0.0 copy-done.1
  285.7 1.0 add.7
  (2 shorter events, 0.0 us)
Async XLA Ops:
  1.7 2.9 copy-start.2
  276.8 2.9 copy-start.3
  281.3 4.4 %copy-start = (f32[3,512,128]{2,1,0:T(8,128)S(1)}, f32[3,512,128]{2,1,0:T(8,128)}, u32[]{:S(2)}) copy-start(f32[3,512,128]{2,1,0:T(8,128)} %param.7) | copy-start | bytes 2359300
  281.3 4.4 %copy-start.1 = (f32[3,512,128]{2,1,0:T(8,128)S(1)}, f32[3,512,128]{2,1,0:T(8,128)}, u32[]{:S(2)}) copy-start(f32[3,512,128]{2,1,0:T(8,128)} %get-tuple-element.5) | copy-start | bytes 2359300

commit v3 on v1

--- a/solution.py
+++ b/solution.py
@@ -1,6 +1,8 @@
 import jax
 import jax.numpy as jnp
 from jax import lax
+from jax.experimental import pallas as pl
+from jax.experimental.pallas import tpu as pltpu
 from jax.sharding import PartitionSpec as P
 
 
@@ -9,7 +11,7 @@
     return jnp.repeat(listed.astype(jnp.float32), tile_rows, axis=1)
 
 
-def on_device(resident_inverse, factor, diag_inverse, anc_tiles, slot_tile):
+def plain(resident_inverse, factor, diag_inverse, anc_tiles, slot_tile):
     own_rows, own_cols = resident_inverse.shape
     supers, _, part_width = factor.shape
     row_index = lax.axis_index("row")
@@ -77,6 +79,487 @@
         step *= 2
     return (jnp.stack(news), diag_inverse + totals)
 
+MESH = pl.DeviceIdType.MESH
+BF = jnp.bfloat16
+F32 = jnp.float32
+CORES = 2
+SIDE = 2
+CHIPS = SIDE * SIDE
+DEPTH = 3
+
+
+def sweep(row_count, col_count, supers, factor_ref, matrix_ref, mask_ref, y_out, t_out,
+          y_ref, t_ref, slab, parts, to_core, from_core, to_chip, from_chip, bank, own_y, to_sum, from_sum, all_sum,
+          slab_sem, own_sem, out_sem, ag_send, ag_recv, core_send, core_recv, chip_send, chip_recv,
+          col_send, col_recv, row_send, row_recv, sum_send, sum_recv, all_send, all_recv, go):
+    row = lax.axis_index("row")
+    col = lax.axis_index("col")
+    last = col_count - 1
+    core = row % CORES
+    chip = row // CORES
+    x, y = chip % SIDE, chip // SIDE
+    half = col // 2
+    width = parts.shape[2]
+    piece = slab.shape[2]
+    owners = row_count // CORES
+    passes = col_count * supers
+
+    end = (col == 0) | (col == last)
+
+    def plan(p):
+        late = p // (2 * supers)
+        e = p - 2 * supers
+        tail = e // (2 * (supers - 1))
+        order = (1 - tail) * (2 + e // (supers - 1)) + tail * (e - 2 * (supers - 2))
+        which = (1 - tail) * (e % (supers - 1)) + tail * (supers - 1)
+        return (1 - late) * (p // supers) + late * order, (1 - late) * (p % supers) + late * which
+
+    def place(o):
+        far, odd = o // 2, o % 2
+        return (1 - far) * (col + odd * (1 - 2 * (col % 2))) + far * ((2 - half) + odd * (1 - 2 * half))
+
+    barrier = pltpu.get_barrier_semaphore()
+
+    @pl.loop(1, row_count)
+    def _(by):
+        pl.semaphore_signal(barrier, inc=1, device_id=((row + by) % row_count, col), device_id_type=MESH)
+
+    @pl.loop(1, col_count)
+    def _(by):
+        pl.semaphore_signal(barrier, inc=1, device_id=(row, (col + by) % col_count), device_id_type=MESH)
+
+    def to(src, dst, send, recv, r, c):
+        return pltpu.make_async_remote_copy(
+            src_ref=src, dst_ref=dst, send_sem=send, recv_sem=recv, device_id=(r, c), device_id_type=MESH
+        )
+
+    def landed(ref, sem):
+        pltpu.make_async_copy(ref, ref, sem).wait()
+
+    def part(s, w):
+        return parts.at[s, w]
+
+    def gather(s, w, way, src):
+        return to(src, part(s, w), ag_send.at[way, s, w], ag_recv.at[s, w], row, col + (1 - 2 * way))
+
+    def chip_at(k):
+        xk = (x + 1 - k // 2) % 2
+        yk = (y + 1 - k % 2) % 2
+        return yk * SIDE + xk
+
+    per_pass = 2 * CHIPS
+
+    def slab_copy(step):
+        j = step % per_pass
+        end, begun = j // (per_pass - 1), (j + per_pass - 1) // per_pass
+        even = 1 - j % 2
+        own = end + (1 - end) * even * begun
+        k = (1 - end) * ((1 - even) * ((j + 1) // 2) + even * (j // 2 - begun)) + end * (CHIPS - 1)
+        which = chip_at(k) * CORES + (core + 1 - own) % CORES
+        off = pl.multiple_of(which * piece, piece)
+        slot = step % DEPTH
+        return pltpu.make_async_copy(matrix_ref.at[:, pl.ds(off, piece)], slab.at[slot], slab_sem.at[slot])
+
+    def next_slab(step):
+        slot = step % DEPTH
+        landed(slab.at[slot], slab_sem.at[slot])
+
+        @pl.when(step + DEPTH - 1 < passes * per_pass)
+        def _():
+            slab_copy(step + DEPTH - 1).start()
+
+        return slot
+
+    def load(s):
+        return pltpu.make_async_copy(factor_ref.at[s], y_ref.at[s], own_sem.at[s])
+
+    @pl.loop(0, supers)
+    def _(s):
+        load(s).start()
+
+    for step in range(DEPTH - 1):
+        slab_copy(step).start()
+
+    def own_part(s):
+        landed(y_ref.at[s], own_sem.at[s])
+        parts[s, col] = (y_ref[s].astype(F32).T * mask_ref[s]).astype(BF)
+
+    def send_own(s):
+        @pl.when(col < last)
+        def _():
+            gather(s, col, 0, part(s, col)).start()
+
+        @pl.when(col > 0)
+        def _():
+            gather(s, col, 1, part(s, col)).start()
+
+    own_part(0)
+    pl.semaphore_wait(barrier, row_count - 1 + last)
+
+    @pl.loop(1, supers)
+    def _(s):
+        send_own(s - 1)
+        own_part(s)
+
+    send_own(supers - 1)
+
+    def arrive(d, s):
+        @pl.when(col >= d)
+        def _():
+            landed(part(s, col - d), ag_recv.at[s, col - d])
+
+        @pl.when(col + d <= last)
+        def _():
+            landed(part(s, col + d), ag_recv.at[s, col + d])
+
+    def forward(d, s):
+        @pl.when((col >= d) & (col < last))
+        def _():
+            gather(s, col - d, 0, part(s, col - d)).start()
+
+        @pl.when((col + d <= last) & (col > 0))
+        def _():
+            gather(s, col + d, 1, part(s, col + d)).start()
+
+    def core_copy(p, k):
+        return to(to_core.at[p % 2, k], from_core.at[p, k], core_send.at[p % 2, k], core_recv.at[p, k],
+                  chip * CORES + 1 - core, col)
+
+    def chip_copy(p, k):
+        return to(to_chip.at[p % 2, k], from_chip.at[p, k], chip_send.at[p % 2, k], chip_recv.at[p, k],
+                  chip_at(k) * CORES + core, col)
+
+    def finish(p):
+        o, s = plan(p)
+        total = to_chip[p % 2, CHIPS - 1].astype(F32)
+        for k in range(CHIPS - 1):
+            landed(from_chip.at[p, k], chip_recv.at[p, k])
+            total = total + from_chip[p, k].astype(F32)
+        bank[s, o] = total.astype(BF)
+
+    def col_copy(s, o):
+        return to(bank.at[s, o], bank.at[s, col_count + col], col_send.at[s, o], col_recv.at[s, col], row, place(o))
+
+    def row_copy(s, o, act):
+        c = place(o)
+        dest = CORES * c + row // owners
+        q = row % owners
+        src = bank.at[s, ((o + col_count - 1) // col_count) * (col_count + c)]
+        remote = to(src, own_y.at[s, q], row_send.at[s, o], row_recv.at[s, q], dest, col)
+        if act == "start":
+            @pl.when(o > 0)
+            def _():
+                landed(src, col_recv.at[s, c])
+
+            @pl.when(dest != row)
+            def _():
+                remote.start()
+
+            @pl.when(dest == row)
+            def _():
+                pltpu.make_async_copy(src, own_y.at[s, q], row_recv.at[s, q]).start()
+        else:
+            @pl.when(dest != row)
+            def _():
+                remote.wait_send()
+
+    @pl.loop(0, passes)
+    def _(p):
+        o, s = plan(p)
+        w = place(o)
+
+        @pl.when(o > 0)
+        def _():
+            for d in range(1, col_count):
+                @pl.when(o == d)
+                def _():
+                    arrive(d, s)
+
+                    if d == 1:
+                        @pl.when(s < supers - 1)
+                        def _():
+                            forward(1, s)
+                    if d == 2:
+                        forward(2, s)
+
+                        @pl.when(s == supers - 2)
+                        def _():
+                            forward(1, supers - 1)
+
+        @pl.when((p == passes - 1) & end)
+        def _():
+            for c in range(1, last):
+                pl.semaphore_signal(go, inc=1, device_id=(row, c), device_id_type=MESH)
+
+        @pl.when(p >= 2)
+        def _():
+            finish(p - 2)
+
+        @pl.loop(0, CHIPS + 1)
+        def _(k):
+            @pl.when((k == 1) & (p >= 2))
+            def _():
+                before, which = plan(p - 2)
+
+                @pl.when(before == 0)
+                def _():
+                    row_copy(which, 0, "start")
+
+                @pl.when(((before == 1) & end) | (before == 2))
+                def _():
+                    col_copy(which, before).start()
+
+            @pl.when((k == 1) & (p == passes - 1) & end)
+            def _():
+                @pl.loop(0, supers - 1)
+                def _(e):
+                    col_copy(e, 3).start()
+
+            @pl.when(k < CHIPS)
+            def _():
+                @pl.when(p >= 2)
+                def _():
+                    core_copy(p - 2, k).wait_send()
+
+                slot = next_slab(p * per_pass + 2 * k - (k + CHIPS - 1) // CHIPS)
+
+                @pl.when(k == 1)
+                def _():
+                    core_copy(p, 0).start()
+
+                to_core[p % 2, k] = jnp.dot(parts[s, w], slab[slot], preferred_element_type=F32).astype(BF)
+
+                @pl.when(k >= 2)
+                def _():
+                    chip_copy(p, k - 2).start()
+
+            @pl.when(k > 0)
+            def _():
+                slot = next_slab(p * per_pass + 2 * k - k // CHIPS)
+
+                @pl.when(k < CHIPS)
+                def _():
+                    core_copy(p, k).start()
+
+                @pl.when(k == CHIPS)
+                def _():
+                    chip_copy(p, CHIPS - 2).start()
+
+                @pl.when((p >= 2) & (k < CHIPS))
+                def _():
+                    chip_copy(p - 2, k - 1).wait_send()
+
+                mine = jnp.dot(parts[s, w], slab[slot], preferred_element_type=F32)
+                landed(from_core.at[p, k - 1], core_recv.at[p, k - 1])
+                to_chip[p % 2, k - 1] = (mine + from_core[p, k - 1].astype(F32)).astype(BF)
+
+    def sum_copy(s, by):
+        r = (row + by) % row_count
+        return to(to_sum.at[s, r], from_sum.at[s, row], sum_send.at[s, r], sum_recv.at[s, row], r, col)
+
+    def all_copy(s, by):
+        r = (row + by) % row_count
+        return to(all_sum.at[s, row], all_sum.at[s, row], all_send.at[s, r], all_recv.at[s, row], r, col)
+
+    def out_copy(s):
+        return pltpu.make_async_copy(y_ref.at[s], y_out.at[s], out_sem.at[0, s])
+
+    def sum_out(s):
+        return pltpu.make_async_copy(all_sum.at[s], t_out.at[s], out_sem.at[1, s])
+
+    def settle(s):
+        t_ref[...] = jnp.zeros(t_ref.shape, F32)
+        for q in range(owners):
+            landed(own_y.at[s, q], row_recv.at[s, q])
+            here = own_y[s, q]
+            off = q * piece
+            mine = parts[s, :, :, pl.ds(off, piece)].reshape(t_ref.shape[0], piece)
+            t_ref[...] += lax.dot_general(mine, here, (((1,), (1,)), ((), ())), preferred_element_type=F32)
+        to_sum[s] = t_ref[...].reshape(to_sum.shape[1:]).astype(BF)
+        for q in range(owners):
+            off = q * piece
+            y_ref[s, pl.ds(off, piece), :] = (
+                own_y[s, q].astype(F32) * mask_ref[s, :, pl.ds(off, piece)]
+            ).T.astype(BF)
+
+        @pl.loop(1, row_count)
+        def _(by):
+            sum_copy(s, by).start()
+
+        out_copy(s).start()
+
+    def add_up(s):
+        @pl.loop(1, row_count)
+        def _(by):
+            r = (row + by) % row_count
+            landed(from_sum.at[s, r], sum_recv.at[s, r])
+
+        from_sum[s, row] = to_sum[s, row]
+        total = from_sum[s, 0].astype(F32)
+        for r in range(1, row_count):
+            total = total + from_sum[s, r].astype(F32)
+        all_sum[s, row] = total.astype(BF)
+
+        @pl.loop(1, row_count)
+        def _(by):
+            all_copy(s, by).start()
+
+    def collect(s):
+        @pl.loop(1, row_count)
+        def _(by):
+            r = (row + by) % row_count
+            landed(all_sum.at[s, r], all_recv.at[s, r])
+
+        sum_out(s).start()
+
+    finish(passes - 2)
+
+    @pl.when(end)
+    def _():
+        col_copy(supers - 1, 2).start()
+
+    finish(passes - 1)
+
+    @pl.when(end)
+    def _():
+        col_copy(supers - 1, 3).start()
+
+    @pl.when(jnp.logical_not(end))
+    def _():
+        col_copy(supers - 1, 2).start()
+
+    @pl.loop(0, supers)
+    def _(s):
+        row_copy(s, 1, "start")
+
+    @pl.loop(0, 2 * (supers - 1))
+    def _(i):
+        row_copy(i // 2, 2 + i % 2, "start")
+
+    @pl.when(jnp.logical_not(end))
+    def _():
+        pl.semaphore_wait(go, 2)
+
+        @pl.loop(0, 2 * supers)
+        def _(i):
+            col_copy(i % supers, 1 + 2 * (i // supers)).start()
+
+    settle(0)
+    for o in (2, 3):
+        row_copy(supers - 1, o, "start")
+
+    @pl.loop(1, supers - 1)
+    def _(s):
+        settle(s)
+
+    @pl.loop(0, supers - 1)
+    def _(s):
+        add_up(s)
+
+    settle(supers - 1)
+
+    @pl.loop(0, supers - 1)
+    def _(s):
+        collect(s)
+
+    add_up(supers - 1)
+    collect(supers - 1)
+
+    @pl.loop(0, supers)
+    def _(s):
+        out_copy(s).wait()
+        sum_out(s).wait()
+
+        @pl.loop(1, row_count)
+        def _(by):
+            sum_copy(s, by).wait_send()
+            all_copy(s, by).wait_send()
+
+        @pl.loop(0, col_count)
+        def _(w):
+            @pl.when((w <= col) & (col < last))
+            def _():
+                gather(s, w, 0, part(s, w)).wait_send()
+
+            @pl.when((w >= col) & (col > 0))
+            def _():
+                gather(s, w, 1, part(s, w)).wait_send()
+
+    @pl.loop(0, passes)
+    def _(p):
+        s, o = p // col_count, p % col_count
+        row_copy(s, o, "wait")
+
+        @pl.when(o > 0)
+        def _():
+            col_copy(s, o).wait_send()
+
+        @pl.when(p >= passes - 2)
+        def _():
+            @pl.loop(0, CHIPS)
+            def _(k):
+                core_copy(p, k).wait_send()
+
+                @pl.when(k < CHIPS - 1)
+                def _():
+                    chip_copy(p, k).wait_send()
+
+
+def fused(resident_inverse, factor, diag_inverse, anc_tiles, slot_tile):
+    own_rows, own_cols = resident_inverse.shape
+    supers, _, width = factor.shape
+    row_count, col_count = lax.axis_size("row"), lax.axis_size("col")
+    total_rows = own_rows * row_count
+    row_mask = slot_rows(anc_tiles, slot_tile, total_rows // slot_tile.shape[0])
+    own_mask = lax.dynamic_slice_in_dim(row_mask, lax.axis_index("row") * own_rows, own_rows, 1)
+    piece = own_cols // row_count
+    owners = row_count // CORES
+    passes = col_count * supers
+    wide = width * col_count
+    dma = pltpu.SemaphoreType.DMA
+    y, t = pl.pallas_call(
+        lambda *refs: sweep(row_count, col_count, supers, *refs),
+        out_shape=(
+            jax.ShapeDtypeStruct((supers, own_rows, width), BF),
+            jax.ShapeDtypeStruct((supers, row_count, wide // row_count, width), BF),
+        ),
+        in_specs=[pl.BlockSpec(memory_space=pl.ANY)] * 2 + [pl.BlockSpec(memory_space=pltpu.VMEM)],
+        out_specs=[pl.BlockSpec(memory_space=pl.ANY)] * 2,
+        scratch_shapes=[
+            pltpu.VMEM((supers, own_rows, width), BF),
+            pltpu.VMEM((wide, width), F32),
+            pltpu.VMEM((DEPTH, own_rows, piece), BF),
+            pltpu.VMEM((supers, col_count, width, own_rows), BF),
+            pltpu.VMEM((2, CHIPS, width, piece), BF),
+            pltpu.VMEM((passes, CHIPS, width, piece), BF),
+            pltpu.VMEM((2, CHIPS, width, piece), BF),
+            pltpu.VMEM((passes, CHIPS - 1, width, piece), BF),
+            pltpu.VMEM((supers, 2 * col_count, width, piece), BF),
+            pltpu.VMEM((supers, owners, width, piece), BF),
+            pltpu.VMEM((supers, row_count, wide // row_count, width), BF),
+            pltpu.VMEM((supers, row_count, wide // row_count, width), BF),
+            pltpu.VMEM((supers, row_count, wide // row_count, width), BF),
+            dma((DEPTH,)), dma((supers,)), dma((2, supers)),
+            dma((2, supers, col_count)), dma((supers, col_count)),
+            dma((2, CHIPS)), dma((passes, CHIPS)),
+            dma((2, CHIPS)), dma((passes, CHIPS)),
+            dma((supers, col_count)), dma((supers, col_count)),
+            dma((supers, col_count)), dma((supers, owners)),
+            dma((supers, row_count)), dma((supers, row_count)),
+            dma((supers, row_count)), dma((supers, row_count)),
+            pltpu.SemaphoreType.REGULAR,
+        ],
+        compiler_params=pltpu.CompilerParams(
+            collective_id=0, has_side_effects=True, vmem_limit_bytes=67043328
+        ),
+    )(factor, resident_inverse, own_mask[:, None, :])
+    return (-y, diag_inverse + t.reshape(diag_inverse.shape).astype(F32))
+
+
+def on_device(*arrays):
+    square = lax.axis_size("row") == CHIPS * CORES and lax.axis_size("col") == CHIPS
+    return (fused if square else plain)(*arrays)
+
 
 def solution(mesh):
     placed = (P("row", "col"), P(None, "row", "col"), P(None, None, "col"), P(), P())

time: 440 us -> 252 us (0.57); the launches traced: 431 us -> 251 us
  Pallas kernels: 0 us -> 244 us
  waiting for transfers between devices: 190 us -> 0 us
  starting transfers between devices: 101 us -> 0 us
  matrix products: 83.7 us -> 0 us
  local copies, waits for them, and re-layouts: 24.4 us -> 0.98 us
  between operations: 15.1 us -> 0.69 us
  other arithmetic: 17.2 us -> 5.43 us
    pallas_call x0 -> x1, Pallas kernels: none -> 244 us  [fused(): pl.pallas_call(lambda *refs: sweep(row_count, col_count, supers, *refs),...]
    ppermute x42 -> x0, waiting for transfers between devices: 141 us -> none  [the longest x9 112 us: on_device(): downs.append(lax.ppermute(downs[-1], 'col', down_moves))]
    ppermute x42 -> x0, starting transfers between devices: 100 us -> none  [the longest x9 44 us: on_device(): ups.append(lax.ppermute(ups[-1], 'col', up_moves))]
    dot_general x15 -> x0, matrix products: 83.7 us -> none  [the longest x3 78.8 us: on_device(): lax.dot_general(resident_inverse, wide, (((0,), (0,)), ((), ())), preferr...]
    reduce_scatter x3 -> x0, waiting for transfers between devices: 49 us -> none  [on_device(): summed = lax.psum_scatter(partial, 'row', scatter_dimension=0, tiled=True)]
    dynamic_slice x17 -> x1, local copies, waits for them, and re-layouts: 9.5 us -> 0.02 us  [fused(): lax.dynamic_slice_in_dim(row_mask, lax.axis_index('row') * own_rows, own_...]
    unnamed x46 -> x6, local copies, waits for them, and re-layouts: 8.35 us -> 0.32 us
    another operation x12 -> x0, other arithmetic: 7.87 us -> none  [the longest x3 3.46 us: on_device(): got = jnp.stack(got)]
  transfers between devices with their start and end apart: 45 -> 0, of which waited for: 17 -> 0; matrix products, arithmetic and copies ran while one was open for 19% -> 0% of each run, Pallas kernels for 0% -> 0%
where the time goes in v3:
time: 252 us; the launch traced here: 251 us
  Pallas kernels  244 us (97%)
  other arithmetic  5.43 us (2%)
    pallas_call x1, Pallas kernels, fused(): pl.pallas_call(lambda *refs: sweep(row_count, col_count, supers, *refs),...  244 us

profile of v3, /device:TPU:0, one launch (start us, length us, event | category | flops | bytes accessed | tf_op | source)
XLA Modules:
  0.0 251.4 jit_solution(13820825122529690928)
XLA Ops:
  0.6 0.8 compare_reduce_fusion
  1.4 0.1 broadcast_bitcast_fusion
  1.6 0.2 copy.7
  1.8 0.6 broadcast_in_dim.9.refs_2_
  2.4 244.3 %shard_map.68 = (bf16[3,3072,128]{2,1,0:T(8,128)(2,1)}, bf16[3,8,64,128]{3,2,1,0:T(8,128)(2,1)}) custom-call(bf16[3,3072,128]{2,1,0:T(8,128)(2,1)} %refs_0_.1, bf16[3072,6144]{1,0:T(8,128)(2,1)} %refs_1_.1, f32[3,1,3072]{2,1,0:T(1,128)} %broadcast_in_dim.9.refs_2_), custom_call_target="tpu_custom_call" | custom-call | tf_op jit(solution)/shard_map/pallas_call | solution.py:520
  246.8 0.0 copy-start
  246.8 0.0 copy-start.1
  246.8 3.6 %neg.3 = bf16[3,3072,128]{2,1,0:T(8,128)(2,1)} negate(bf16[3,3072,128]{2,1,0:T(8,128)(2,1)} %get-tuple-element.4) | non-fusion elementwise | flops 1179648 | bytes 4718592 | tf_op jit(solution)/shard_map/neg | solution.py:556
  250.4 0.0 copy-done
  250.4 0.0 copy-done.1
  250.4 1.0 convert_add_fusion
  (2 shorter events, 0.0 us)
Async XLA Ops:
  246.8 3.6 %copy-start = (f32[3,512,128]{2,1,0:T(8,128)S(1)}, f32[3,512,128]{2,1,0:T(8,128)}, u32[]{:S(2)}) copy-start(f32[3,512,128]{2,1,0:T(8,128)} %param.7) | copy-start | bytes 2359300
  246.8 3.6 %copy-start.1 = (bf16[3,8,64,128]{3,2,1,0:T(8,128)(2,1)S(1)}, bf16[3,8,64,128]{3,2,1,0:T(8,128)(2,1)}, u32[]{:S(2)}) copy-start(bf16[3,8,64,128]{3,2,1,0:T(8,128)(2,1)} %get-tuple-element.5) | copy-start | bytes 1179652

commit v4 on v3

--- a/solution.py
+++ b/solution.py
@@ -268,6 +268,12 @@
         o, s = plan(p)
         w = place(o)
 
+        @pl.when((p == passes - 1) & end)
+        def _():
+            row_copy(supers - 1, 1, "start")
+            row_copy(0, 2, "start")
+            row_copy(0, 3, "start")
+
         @pl.when(o > 0)
         def _():
             for d in range(1, col_count):
@@ -305,13 +311,17 @@
                 def _():
                     row_copy(which, 0, "start")
 
-                @pl.when(((before == 1) & end) | (before == 2))
+                @pl.when((before == 1) | (before == 2) | ((before == 3) & (which == 0)))
                 def _():
                     col_copy(which, before).start()
 
+            @pl.when((k == 2) & (p >= passes - 1 - supers) & (p < passes - 2) & end)
+            def _():
+                row_copy(p - (passes - 1 - supers), 1, "start")
+
             @pl.when((k == 1) & (p == passes - 1) & end)
             def _():
-                @pl.loop(0, supers - 1)
+                @pl.loop(1, supers - 1)
                 def _(e):
                     col_copy(e, 3).start()
 
@@ -379,7 +389,7 @@
         for q in range(owners):
             off = q * piece
             y_ref[s, pl.ds(off, piece), :] = (
-                own_y[s, q].astype(F32) * mask_ref[s, :, pl.ds(off, piece)]
+                own_y[s, q].astype(F32) * -mask_ref[s, :, pl.ds(off, piece)]
             ).T.astype(BF)
 
         @pl.loop(1, row_count)
@@ -412,11 +422,55 @@
 
         sum_out(s).start()
 
+    def drain_early():
+        @pl.loop(0, supers)
+        def _(s):
+            @pl.loop(0, col_count)
+            def _(w):
+                @pl.when((w <= col) & (col < last))
+                def _():
+                    gather(s, w, 0, part(s, w)).wait_send()
+
+                @pl.when((w >= col) & (col > 0))
+                def _():
+                    gather(s, w, 1, part(s, w)).wait_send()
+
+        @pl.loop(passes - 2, passes)
+        def _(p):
+            @pl.loop(0, CHIPS)
+            def _(k):
+                core_copy(p, k).wait_send()
+
+                @pl.when(k < CHIPS - 1)
+                def _():
+                    chip_copy(p, k).wait_send()
+
+    def drain(s):
+        @pl.loop(0, col_count)
+        def _(o):
+            row_copy(s, o, "wait")
+
+            @pl.when(o > 0)
+            def _():
+                col_copy(s, o).wait_send()
+
+        @pl.loop(1, row_count)
+        def _(by):
+            sum_copy(s, by).wait_send()
+
+        out_copy(s).wait()
+
     finish(passes - 2)
+
+    def middle_rows():
+        @pl.loop(2, 2 * (supers - 1))
+        def _(i):
+            row_copy(i // 2, 2 + i % 2, "start")
 
     @pl.when(end)
     def _():
         col_copy(supers - 1, 2).start()
+        middle_rows()
 
     finish(passes - 1)
 
@@ -428,27 +482,29 @@
     def _():
         col_copy(supers - 1, 2).start()
 
-    @pl.loop(0, supers)
-    def _(s):
-        row_copy(s, 1, "start")
-
-    @pl.loop(0, 2 * (supers - 1))
-    def _(i):
-        row_copy(i // 2, 2 + i % 2, "start")
+        @pl.loop(0, supers)
+        def _(s):
+            row_copy(s, 1, "start")
+
+        row_copy(0, 2, "start")
+        row_copy(0, 3, "start")
+        middle_rows()
+
+    drain_early()
 
     @pl.when(jnp.logical_not(end))
     def _():
         pl.semaphore_wait(go, 2)
 
-        @pl.loop(0, 2 * supers)
-        def _(i):
-            col_copy(i % supers, 1 + 2 * (i // supers)).start()
+        @pl.loop(1, supers)
+        def _(s):
+            col_copy(s, 3).start()
 
     settle(0)
     for o in (2, 3):
         row_copy(supers - 1, o, "start")
 
-    @pl.loop(1, supers - 1)
+    @pl.loop(1, supers)
     def _(s):
         settle(s)
 
@@ -456,53 +512,48 @@
     def _(s):
         add_up(s)
 
-    settle(supers - 1)
+    add_up(supers - 1)
 
     @pl.loop(0, supers - 1)
     def _(s):
         collect(s)
 
-    add_up(supers - 1)
-    collect(supers - 1)
-
     @pl.loop(0, supers)
     def _(s):
-        out_copy(s).wait()
-        sum_out(s).wait()
-
+        drain(s)
+
+    collect(supers - 1)
+
+    @pl.loop(0, supers)
+    def _(s):
         @pl.loop(1, row_count)
         def _(by):
-            sum_copy(s, by).wait_send()
             all_copy(s, by).wait_send()
 
-        @pl.loop(0, col_count)
-        def _(w):
-            @pl.when((w <= col) & (col < last))
-            def _():
-                gather(s, w, 0, part(s, w)).wait_send()
-
-            @pl.when((w >= col) & (col > 0))
-            def _():
-                gather(s, w, 1, part(s, w)).wait_send()
-
-    @pl.loop(0, passes)
-    def _(p):
-        s, o = p // col_count, p % col_count
-        row_copy(s, o, "wait")
-
-        @pl.when(o > 0)
-        def _():
-            col_copy(s, o).wait_send()
-
-        @pl.when(p >= passes - 2)
-        def _():
-            @pl.loop(0, CHIPS)
-            def _(k):
-                core_copy(p, k).wait_send()
-
-                @pl.when(k < CHIPS - 1)
-                def _():
-                    chip_copy(p, k).wait_send()
+        sum_out(s).wait()
+
+
+def close(y_ref, t_ref, diag_ref, new_ref, out_ref, y, t, diag, y_sem, t_sem, diag_sem, new_sem, out_sem):
+    supers = y_ref.shape[0]
+
+    def copy(src, dst, sem):
+        return pltpu.make_async_copy(src, dst, sem)
+
+    t_in, diag_in = copy(t_ref, t, t_sem), copy(diag_ref, diag, diag_sem)
+    y_in = [copy(y_ref.at[s], y.at[s], y_sem.at[s]) for s in range(supers)]
+    y_over = [copy(y.at[s], new_ref.at[s], new_sem.at[s]) for s in range(supers)]
+    for each in y_in + [t_in, diag_in]:
+        each.start()
+    for s in range(supers):
+        y_in[s].wait()
+        y_over[s].start()
+    t_in.wait()
+    diag_in.wait()
+    diag[...] += t[...].astype(F32)
+    over = copy(diag, out_ref, out_sem)
+    over.start()
+    for each in y_over + [over]:
+        each.wait()
 
 
 def fused(resident_inverse, factor, diag_inverse, anc_tiles, slot_tile):
@@ -553,7 +604,17 @@
             collective_id=0, has_side_effects=True, vmem_limit_bytes=67043328
         ),
     )(factor, resident_inverse, own_mask[:, None, :])
-    return (-y, diag_inverse + t.reshape(diag_inverse.shape).astype(F32))
+    t = t.reshape(diag_inverse.shape)
+    return tuple(pl.pallas_call(
+        close,
+        in_specs=[pl.BlockSpec(memory_space=pl.ANY)] * 3,
+        out_specs=[pl.BlockSpec(memory_space=pl.ANY)] * 2,
+        out_shape=(jax.ShapeDtypeStruct(y.shape, BF), jax.ShapeDtypeStruct(t.shape, F32)),
+        scratch_shapes=[
+            pltpu.VMEM(y.shape, BF), pltpu.VMEM(t.shape, BF), pltpu.VMEM(t.shape, F32),
+            dma((supers,)), dma(()), dma(()), dma((supers,)), dma(()),
+        ],
+    )(y, t, diag_inverse))
 
 
 def on_device(*arrays):

time: 252 us -> 235 us (0.933)
  Pallas kernels: 244 us -> 232 us
  other arithmetic: 5.43 us -> 0.81 us
    pallas_call x1, Pallas kernels: 244 us -> 229 us  [fused(): pl.pallas_call(lambda *refs: sweep(row_count, col_count, supers, *refs),...]
    neg x1 -> x0, other arithmetic: 3.62 us -> none  [fused(): return (-y, diag_inverse + t.reshape(diag_inverse.shape).astype(F32))]
    pallas_call x0 -> x1, Pallas kernels: none -> 2.99 us  [fused(): pl.pallas_call(close, in_specs=[pl.BlockSpec(memory_space=pl.ANY)] * 3, o...]
where the time goes in v4:
time: 235 us; the launch traced here: 234 us
  Pallas kernels  232 us (99%)
    pallas_call x1, Pallas kernels, fused(): pl.pallas_call(lambda *refs: sweep(row_count, col_count, supers, *refs),...  229 us

profile of v4, /device:TPU:0, one launch (start us, length us, event | category | flops | bytes accessed | tf_op | source)
XLA Modules:
  0.0 234.4 jit_solution(11542504105783843709)
XLA Ops:
  0.6 0.8 compare_reduce_fusion
  1.4 0.1 broadcast_bitcast_fusion
  1.6 0.2 copy.7
  1.8 0.6 broadcast_in_dim.9.refs_2_
  2.4 229.0 %shard_map.68 = (bf16[3,3072,128]{2,1,0:T(8,128)(2,1)}, bf16[3,8,64,128]{3,2,1,0:T(8,128)(2,1)}) custom-call(bf16[3,3072,128]{2,1,0:T(8,128)(2,1)} %refs_0_.1, bf16[3072,6144]{1,0:T(8,128)(2,1)} %refs_1_.1, f32[3,1,3072]{2,1,0:T(1,128)} %broadcast_in_dim.9.refs_2_), custom_call_target="tpu_custom_call" | custom-call | tf_op jit(solution)/shard_map/pallas_call | solution.py:571
  231.5 3.0 %shard_map.69 = (bf16[3,3072,128]{2,1,0:T(8,128)(2,1)}, f32[3,512,128]{2,1,0:T(8,128)}) custom-call(bf16[3,3072,128]{2,1,0:T(8,128)(2,1)} %get-tuple-element.4.y_ref, bf16[3,512,128]{2,1,0:T(8,128)(2,1)} %bitcast.5, f32[3,512,128]{2,1,0:T(8,128)} %diag_ref.1), custom_call_target="tpu_custom_call" | custom-call | tf_op jit(solution)/shard_map/pallas_call | solution.py:608
  (2 shorter events, 0.0 us)

commit v5 on v4

--- a/solution.py
+++ b/solution.py
@@ -85,7 +85,7 @@
 CORES = 2
 SIDE = 2
 CHIPS = SIDE * SIDE
-DEPTH = 3
+DEPTH = 4
 
 
 def sweep(row_count, col_count, supers, factor_ref, matrix_ref, mask_ref, y_out, t_out,
@@ -143,8 +143,8 @@
         return to(src, part(s, w), ag_send.at[way, s, w], ag_recv.at[s, w], row, col + (1 - 2 * way))
 
     def chip_at(k):
-        xk = (x + 1 - k // 2) % 2
-        yk = (y + 1 - k % 2) % 2
+        xk = (x + 1 - k % 2) % 2
+        yk = (y + 1 - k // 2) % 2
         return yk * SIDE + xk
 
     per_pass = 2 * CHIPS
@@ -163,12 +163,12 @@
     def next_slab(step):
         slot = step % DEPTH
         landed(slab.at[slot], slab_sem.at[slot])
-
-        @pl.when(step + DEPTH - 1 < passes * per_pass)
-        def _():
-            slab_copy(step + DEPTH - 1).start()
-
         return slot
+
+    def refill(step):
+        @pl.when(step + DEPTH < passes * per_pass)
+        def _():
+            slab_copy(step + DEPTH).start()
 
     def load(s):
         return pltpu.make_async_copy(factor_ref.at[s], y_ref.at[s], own_sem.at[s])
@@ -177,7 +177,7 @@
     def _(s):
         load(s).start()
 
-    for step in range(DEPTH - 1):
+    for step in range(DEPTH):
         slab_copy(step).start()
 
     def own_part(s):
@@ -263,6 +263,10 @@
             def _():
                 remote.wait_send()
 
+    def release(turn):
+        for c in range(1, last):
+            pl.semaphore_signal(go.at[turn], inc=1, device_id=(row, c), device_id_type=MESH)
+
     @pl.loop(0, passes)
     def _(p):
         o, s = plan(p)
@@ -270,7 +274,6 @@
 
         @pl.when((p == passes - 1) & end)
         def _():
-            row_copy(supers - 1, 1, "start")
             row_copy(0, 2, "start")
             row_copy(0, 3, "start")
 
@@ -294,8 +297,7 @@
 
         @pl.when((p == passes - 1) & end)
         def _():
-            for c in range(1, last):
-                pl.semaphore_signal(go, inc=1, device_id=(row, c), device_id_type=MESH)
+            release(0)
 
         @pl.when(p >= 2)
         def _():
@@ -311,13 +313,17 @@
                 def _():
                     row_copy(which, 0, "start")
 
-                @pl.when((before == 1) | (before == 2) | ((before == 3) & (which == 0)))
+                @pl.when(((before == 1) & (end | (which < supers - 1))) | (before == 2) | ((before == 3) & (which == 0)))
                 def _():
                     col_copy(which, before).start()
 
             @pl.when((k == 2) & (p >= passes - 1 - supers) & (p < passes - 2) & end)
             def _():
                 row_copy(p - (passes - 1 - supers), 1, "start")
+
+            @pl.when((k == 2) & (p == passes - 1) & end)
+            def _():
+                release(1)
 
             @pl.when((k == 1) & (p == passes - 1) & end)
             def _():
@@ -331,13 +337,15 @@
                 def _():
                     core_copy(p - 2, k).wait_send()
 
-                slot = next_slab(p * per_pass + 2 * k - (k + CHIPS - 1) // CHIPS)
+                step = p * per_pass + 2 * k - (k + CHIPS - 1) // CHIPS
+                slot = next_slab(step)
 
                 @pl.when(k == 1)
                 def _():
                     core_copy(p, 0).start()
 
                 to_core[p % 2, k] = jnp.dot(parts[s, w], slab[slot], preferred_element_type=F32).astype(BF)
+                refill(step)
 
                 @pl.when(k >= 2)
                 def _():
@@ -345,7 +353,8 @@
 
             @pl.when(k > 0)
             def _():
-                slot = next_slab(p * per_pass + 2 * k - k // CHIPS)
+                step = p * per_pass + 2 * k - k // CHIPS
+                slot = next_slab(step)
 
                 @pl.when(k < CHIPS)
                 def _():
@@ -362,6 +371,7 @@
                 mine = jnp.dot(parts[s, w], slab[slot], preferred_element_type=F32)
                 landed(from_core.at[p, k - 1], core_recv.at[p, k - 1])
                 to_chip[p % 2, k - 1] = (mine + from_core[p, k - 1].astype(F32)).astype(BF)
+                refill(step)
 
     def sum_copy(s, by):
         r = (row + by) % row_count
@@ -386,16 +396,21 @@
             mine = parts[s, :, :, pl.ds(off, piece)].reshape(t_ref.shape[0], piece)
             t_ref[...] += lax.dot_general(mine, here, (((1,), (1,)), ((), ())), preferred_element_type=F32)
         to_sum[s] = t_ref[...].reshape(to_sum.shape[1:]).astype(BF)
-        for q in range(owners):
+
+        def write(q):
             off = q * piece
             y_ref[s, pl.ds(off, piece), :] = (
                 own_y[s, q].astype(F32) * -mask_ref[s, :, pl.ds(off, piece)]
             ).T.astype(BF)
 
+        write(0)
+
         @pl.loop(1, row_count)
         def _(by):
             sum_copy(s, by).start()
 
+        for q in range(1, owners):
+            write(q)
         out_copy(s).start()
 
     def add_up(s):
@@ -494,15 +509,24 @@
 
     @pl.when(jnp.logical_not(end))
     def _():
-        pl.semaphore_wait(go, 2)
-
-        @pl.loop(1, supers)
+        pl.semaphore_wait(go.at[0], 2)
+
+        @pl.loop(1, supers - 1)
         def _(s):
             col_copy(s, 3).start()
 
+        pl.semaphore_wait(go.at[1], 2)
+        col_copy(supers - 1, 3).start()
+        col_copy(supers - 1, 1).start()
+
     settle(0)
-    for o in (2, 3):
-        row_copy(supers - 1, o, "start")
+    row_copy(supers - 1, 2, "start")
+
+    @pl.when(end)
+    def _():
+        row_copy(supers - 1, 1, "start")
+
+    row_copy(supers - 1, 3, "start")
 
     @pl.loop(1, supers)
     def _(s):
@@ -598,7 +622,7 @@
             dma((supers, col_count)), dma((supers, owners)),
             dma((supers, row_count)), dma((supers, row_count)),
             dma((supers, row_count)), dma((supers, row_count)),
-            pltpu.SemaphoreType.REGULAR,
+            pltpu.SemaphoreType.REGULAR((2,)),
         ],
         compiler_params=pltpu.CompilerParams(
             collective_id=0, has_side_effects=True, vmem_limit_bytes=67043328

time: 235 us -> 229 us (0.974)
  Pallas kernels: 232 us -> 226 us
    pallas_call x1, Pallas kernels: 229 us -> 223 us  [fused(): pl.pallas_call(lambda *refs: sweep(row_count, col_count, supers, *refs),...]
where the time goes in v5:
time: 229 us
  Pallas kernels  226 us (99%)
    pallas_call x1, Pallas kernels, fused(): pl.pallas_call(lambda *refs: sweep(row_count, col_count, supers, *refs),...  223 us

profile of v5, /device:TPU:0, one launch (start us, length us, event | category | flops | bytes accessed | tf_op | source)
XLA Modules:
  0.0 228.7 jit_solution(367945094574740835)
XLA Ops:
  0.6 0.8 compare_reduce_fusion
  1.4 0.1 broadcast_bitcast_fusion
  1.6 0.2 copy.7
  1.8 0.6 broadcast_in_dim.9.refs_2_
  2.4 223.3 %shard_map.68 = (bf16[3,3072,128]{2,1,0:T(8,128)(2,1)}, bf16[3,8,64,128]{3,2,1,0:T(8,128)(2,1)}) custom-call(bf16[3,3072,128]{2,1,0:T(8,128)(2,1)} %refs_0_.1, bf16[3072,6144]{1,0:T(8,128)(2,1)} %refs_1_.1, f32[3,1,3072]{2,1,0:T(1,128)} %broadcast_in_dim.9.refs_2_), custom_call_target="tpu_custom_call" | custom-call | tf_op jit(solution)/shard_map/pallas_call | solution.py:595
  225.7 3.0 %shard_map.69 = (bf16[3,3072,128]{2,1,0:T(8,128)(2,1)}, f32[3,512,128]{2,1,0:T(8,128)}) custom-call(bf16[3,3072,128]{2,1,0:T(8,128)(2,1)} %get-tuple-element.4.y_ref, bf16[3,512,128]{2,1,0:T(8,128)(2,1)} %bitcast.5, f32[3,512,128]{2,1,0:T(8,128)} %diag_ref.1), custom_call_target="tpu_custom_call" | custom-call | tf_op jit(solution)/shard_map/pallas_call | solution.py:632
  (2 shorter events, 0.0 us)

commit v6 on v5

--- a/solution.py
+++ b/solution.py
@@ -379,13 +379,13 @@
 
     def all_copy(s, by):
         r = (row + by) % row_count
-        return to(all_sum.at[s, row], all_sum.at[s, row], all_send.at[s, r], all_recv.at[s, row], r, col)
+        return to(all_sum.at[s], t_out.at[s, row], all_send.at[s, r], all_recv.at[s, row], r, col)
 
     def out_copy(s):
         return pltpu.make_async_copy(y_ref.at[s], y_out.at[s], out_sem.at[0, s])
 
     def sum_out(s):
-        return pltpu.make_async_copy(all_sum.at[s], t_out.at[s], out_sem.at[1, s])
+        return pltpu.make_async_copy(all_sum.at[s], t_out.at[s, row], out_sem.at[1, s])
 
     def settle(s):
         t_ref[...] = jnp.zeros(t_ref.shape, F32)
@@ -423,19 +423,19 @@
         total = from_sum[s, 0].astype(F32)
         for r in range(1, row_count):
             total = total + from_sum[s, r].astype(F32)
-        all_sum[s, row] = total.astype(BF)
+        all_sum[s] = total.astype(BF)
 
         @pl.loop(1, row_count)
         def _(by):
             all_copy(s, by).start()
+
+        sum_out(s).start()
 
     def collect(s):
         @pl.loop(1, row_count)
         def _(by):
             r = (row + by) % row_count
-            landed(all_sum.at[s, r], all_recv.at[s, r])
-
-        sum_out(s).start()
+            landed(t_out.at[s, r], all_recv.at[s, r])
 
     def drain_early():
         @pl.loop(0, supers)
@@ -528,11 +528,14 @@
 
     row_copy(supers - 1, 3, "start")
 
-    @pl.loop(1, supers)
+    settle(1)
+    add_up(0)
+
+    @pl.loop(2, supers)
     def _(s):
         settle(s)
 
-    @pl.loop(0, supers - 1)
+    @pl.loop(1, supers - 1)
     def _(s):
         add_up(s)
 
@@ -564,13 +567,15 @@
         return pltpu.make_async_copy(src, dst, sem)
 
     t_in, diag_in = copy(t_ref, t, t_sem), copy(diag_ref, diag, diag_sem)
-    y_in = [copy(y_ref.at[s], y.at[s], y_sem.at[s]) for s in range(supers)]
-    y_over = [copy(y.at[s], new_ref.at[s], new_sem.at[s]) for s in range(supers)]
+    half = y_ref.shape[1] // 2
+    parts = [(s, pl.ds(h * half, half)) for s in range(supers) for h in range(2)]
+    y_in = [copy(y_ref.at[at], y.at[at], y_sem.at[i]) for i, at in enumerate(parts)]
+    y_over = [copy(y.at[at], new_ref.at[at], new_sem.at[i]) for i, at in enumerate(parts)]
     for each in y_in + [t_in, diag_in]:
         each.start()
-    for s in range(supers):
-        y_in[s].wait()
-        y_over[s].start()
+    for came, goes in zip(y_in, y_over):
+        came.wait()
+        goes.start()
     t_in.wait()
     diag_in.wait()
     diag[...] += t[...].astype(F32)
@@ -613,7 +618,7 @@
             pltpu.VMEM((supers, owners, width, piece), BF),
             pltpu.VMEM((supers, row_count, wide // row_count, width), BF),
             pltpu.VMEM((supers, row_count, wide // row_count, width), BF),
-            pltpu.VMEM((supers, row_count, wide // row_count, width), BF),
+            pltpu.VMEM((supers, wide // row_count, width), BF),
             dma((DEPTH,)), dma((supers,)), dma((2, supers)),
             dma((2, supers, col_count)), dma((supers, col_count)),
             dma((2, CHIPS)), dma((passes, CHIPS)),
@@ -636,7 +641,7 @@
         out_shape=(jax.ShapeDtypeStruct(y.shape, BF), jax.ShapeDtypeStruct(t.shape, F32)),
         scratch_shapes=[
             pltpu.VMEM(y.shape, BF), pltpu.VMEM(t.shape, BF), pltpu.VMEM(t.shape, F32),
-            dma((supers,)), dma(()), dma(()), dma((supers,)), dma(()),
+            dma((2 * supers,)), dma(()), dma(()), dma((2 * supers,)), dma(()),
         ],
     )(y, t, diag_inverse))
 

time: 229 us -> 229 us (level)
  no operation moved by 1% of the time
where the time goes in v6:
time: 229 us
  Pallas kernels  227 us (99%)
    pallas_call x1, Pallas kernels, fused(): pl.pallas_call(lambda *refs: sweep(row_count, col_count, supers, *refs),...  224 us

profile of v6, /device:TPU:0, one launch (start us, length us, event | category | flops | bytes accessed | tf_op | source)
XLA Modules:
  0.0 229.1 jit_solution(5040700261046241841)
XLA Ops:
  0.6 0.8 compare_reduce_fusion
  1.4 0.1 broadcast_bitcast_fusion
  1.6 0.2 copy.7
  1.8 0.6 broadcast_in_dim.9.refs_2_
  2.4 223.5 %shard_map.68 = (bf16[3,3072,128]{2,1,0:T(8,128)(2,1)}, bf16[3,8,64,128]{3,2,1,0:T(8,128)(2,1)}) custom-call(bf16[3,3072,128]{2,1,0:T(8,128)(2,1)} %refs_0_.1, bf16[3072,6144]{1,0:T(8,128)(2,1)} %refs_1_.1, f32[3,1,3072]{2,1,0:T(1,128)} %broadcast_in_dim.9.refs_2_), custom_call_target="tpu_custom_call" | custom-call | tf_op jit(solution)/shard_map/pallas_call | solution.py:600
  226.0 3.2 %shard_map.69 = (bf16[3,3072,128]{2,1,0:T(8,128)(2,1)}, f32[3,512,128]{2,1,0:T(8,128)}) custom-call(bf16[3,3072,128]{2,1,0:T(8,128)(2,1)} %get-tuple-element.4.y_ref, bf16[3,512,128]{2,1,0:T(8,128)(2,1)} %bitcast.5, f32[3,512,128]{2,1,0:T(8,128)} %diag_ref.1), custom_call_target="tpu_custom_call" | custom-call | tf_op jit(solution)/shard_map/pallas_call | solution.py:637
  (2 shorter events, 0.0 us)

commit v7 on v6

--- a/solution.py
+++ b/solution.py
@@ -86,6 +86,7 @@
 SIDE = 2
 CHIPS = SIDE * SIDE
 DEPTH = 4
+STRIPS = 2
 
 
 def sweep(row_count, col_count, supers, factor_ref, matrix_ref, mask_ref, y_out, t_out,
@@ -237,31 +238,41 @@
             total = total + from_chip[p, k].astype(F32)
         bank[s, o] = total.astype(BF)
 
-    def col_copy(s, o):
-        return to(bank.at[s, o], bank.at[s, col_count + col], col_send.at[s, o], col_recv.at[s, col], row, place(o))
+    def strip(h):
+        return pl.ds(h * (width // STRIPS), width // STRIPS)
+
+    def col_copy(s, o, h):
+        return to(bank.at[s, o, strip(h)], bank.at[s, col_count + col, strip(h)],
+                  col_send.at[s, o, h], col_recv.at[s, col, h], row, place(o))
+
+    def col_start(s, o):
+        for h in range(STRIPS):
+            col_copy(s, o, h).start()
 
     def row_copy(s, o, act):
         c = place(o)
         dest = CORES * c + row // owners
         q = row % owners
-        src = bank.at[s, ((o + col_count - 1) // col_count) * (col_count + c)]
-        remote = to(src, own_y.at[s, q], row_send.at[s, o], row_recv.at[s, q], dest, col)
-        if act == "start":
-            @pl.when(o > 0)
-            def _():
-                landed(src, col_recv.at[s, c])
-
-            @pl.when(dest != row)
-            def _():
-                remote.start()
-
-            @pl.when(dest == row)
-            def _():
-                pltpu.make_async_copy(src, own_y.at[s, q], row_recv.at[s, q]).start()
-        else:
-            @pl.when(dest != row)
-            def _():
-                remote.wait_send()
+        at = ((o + col_count - 1) // col_count) * (col_count + c)
+        for h in range(STRIPS):
+            src, dst = bank.at[s, at, strip(h)], own_y.at[s, q, strip(h)]
+            remote = to(src, dst, row_send.at[s, o, h], row_recv.at[s, q, h], dest, col)
+            if act == "start":
+                @pl.when(o > 0)
+                def _():
+                    landed(src, col_recv.at[s, c, h])
+
+                @pl.when(dest != row)
+                def _():
+                    remote.start()
+
+                @pl.when(dest == row)
+                def _():
+                    pltpu.make_async_copy(src, dst, row_recv.at[s, q, h]).start()
+            else:
+                @pl.when(dest != row)
+                def _():
+                    remote.wait_send()
 
     def release(turn):
         for c in range(1, last):
@@ -315,7 +326,7 @@
 
                 @pl.when(((before == 1) & (end | (which < supers - 1))) | (before == 2) | ((before == 3) & (which == 0)))
                 def _():
-                    col_copy(which, before).start()
+                    col_start(which, before)
 
             @pl.when((k == 2) & (p >= passes - 1 - supers) & (p < passes - 2) & end)
             def _():
@@ -329,7 +340,7 @@
             def _():
                 @pl.loop(1, supers - 1)
                 def _(e):
-                    col_copy(e, 3).start()
+                    col_start(e, 3)
 
             @pl.when(k < CHIPS)
             def _():
@@ -390,7 +401,8 @@
     def settle(s):
         t_ref[...] = jnp.zeros(t_ref.shape, F32)
         for q in range(owners):
-            landed(own_y.at[s, q], row_recv.at[s, q])
+            for h in range(STRIPS):
+                landed(own_y.at[s, q, strip(h)], row_recv.at[s, q, h])
             here = own_y[s, q]
             off = q * piece
             mine = parts[s, :, :, pl.ds(off, piece)].reshape(t_ref.shape[0], piece)
@@ -467,7 +479,8 @@
 
             @pl.when(o > 0)
             def _():
-                col_copy(s, o).wait_send()
+                for h in range(STRIPS):
+                    col_copy(s, o, h).wait_send()
 
         @pl.loop(1, row_count)
         def _(by):
@@ -484,18 +497,18 @@
 
     @pl.when(end)
     def _():
-        col_copy(supers - 1, 2).start()
+        col_start(supers - 1, 2)
         middle_rows()
 
     finish(passes - 1)
 
     @pl.when(end)
     def _():
-        col_copy(supers - 1, 3).start()
+        col_start(supers - 1, 3)
 
     @pl.when(jnp.logical_not(end))
     def _():
-        col_copy(supers - 1, 2).start()
+        col_start(supers - 1, 2)
 
         @pl.loop(0, supers)
         def _(s):
@@ -513,11 +526,11 @@
 
         @pl.loop(1, supers - 1)
         def _(s):
-            col_copy(s, 3).start()
+            col_start(s, 3)
 
         pl.semaphore_wait(go.at[1], 2)
-        col_copy(supers - 1, 3).start()
-        col_copy(supers - 1, 1).start()
+        col_start(supers - 1, 3)
+        col_start(supers - 1, 1)
 
     settle(0)
     row_copy(supers - 1, 2, "start")
@@ -623,8 +636,8 @@
             dma((2, supers, col_count)), dma((supers, col_count)),
             dma((2, CHIPS)), dma((passes, CHIPS)),
             dma((2, CHIPS)), dma((passes, CHIPS)),
-            dma((supers, col_count)), dma((supers, col_count)),
-            dma((supers, col_count)), dma((supers, owners)),
+            dma((supers, col_count, STRIPS)), dma((supers, col_count, STRIPS)),
+            dma((supers, col_count, STRIPS)), dma((supers, owners, STRIPS)),
             dma((supers, row_count)), dma((supers, row_count)),
             dma((supers, row_count)), dma((supers, row_count)),
             pltpu.SemaphoreType.REGULAR((2,)),

time: 229 us -> 229 us (level)
  no operation moved by 1% of the time
where the time goes in v7:
time: 229 us
  Pallas kernels  227 us (99%)
    pallas_call x1, Pallas kernels, fused(): pl.pallas_call(lambda *refs: sweep(row_count, col_count, supers, *refs),...  224 us

profile of v7, /device:TPU:0, one launch (start us, length us, event | category | flops | bytes accessed | tf_op | source)
XLA Modules:
  0.0 229.2 jit_solution(4171209477127560200)
XLA Ops:
  0.6 0.8 compare_reduce_fusion
  1.4 0.1 broadcast_bitcast_fusion
  1.6 0.2 copy.7
  1.8 0.6 broadcast_in_dim.9.refs_2_
  2.4 223.6 %shard_map.68 = (bf16[3,3072,128]{2,1,0:T(8,128)(2,1)}, bf16[3,8,64,128]{3,2,1,0:T(8,128)(2,1)}) custom-call(bf16[3,3072,128]{2,1,0:T(8,128)(2,1)} %refs_0_.1, bf16[3072,6144]{1,0:T(8,128)(2,1)} %refs_1_.1, f32[3,1,3072]{2,1,0:T(1,128)} %broadcast_in_dim.9.refs_2_), custom_call_target="tpu_custom_call" | custom-call | tf_op jit(solution)/shard_map/pallas_call | solution.py:613
  226.0 3.2 %shard_map.69 = (bf16[3,3072,128]{2,1,0:T(8,128)(2,1)}, f32[3,512,128]{2,1,0:T(8,128)}) custom-call(bf16[3,3072,128]{2,1,0:T(8,128)(2,1)} %get-tuple-element.4.y_ref, bf16[3,512,128]{2,1,0:T(8,128)(2,1)} %bitcast.5, f32[3,512,128]{2,1,0:T(8,128)} %diag_ref.1), custom_call_target="tpu_custom_call" | custom-call | tf_op jit(solution)/shard_map/pallas_call | solution.py:650
  (2 shorter events, 0.0 us)
